TPU v7x, 128 devices: a whole 4x4x4 slice. The times are simulated.
128 devices in a mesh: scan: 32 (over z, y, core), freq: 4 (over x).
Axes of the slice: x: 4, y: 4, z: 4, core: 2. Of those that a mesh axis runs over, the one named last changes fastest.
Arguments:
- frames: float32 [128, 1024, 512], P('freq', 'scan'), may hold values from -6 to 6
- intersection_masks: int32 [128, 128], replicated, may hold values from -1 to 1
- aperture: int32 [128], replicated, may hold values from 0 to 255
- phases: float32 [256], replicated, may hold values from -3.140625 to 3.140625
Outputs:
- ssb_image: float32 [1024, 2, 512], P(('scan', 'freq'))
All inputs are finite; a program needn't handle non-finite values.
Results may differ from a plain program's by a relative error of at most 0.0001.
Values sent between devices are 32-bit elements; how exact they have to be, the bound alone decides.
No kernel may reach another device: no remote copies, remote signals or barrier semaphores. Data moves between devices by JAX's collectives and lax.ppermute only.
A program may use at most 64 MiB of HBM per device.

v0:
```python
import math

import jax
import jax.numpy as jnp
import numpy as np
from jax import lax
from jax.experimental import pallas as pl
from jax.experimental.pallas import tpu as pltpu
from jax.sharding import PartitionSpec as P

AXES = ("scan", "freq")
X0, X1, Y0, Y1, Z0, Z1 = 1, 2, 4, 8, 16, 32
STAGES = (((X0, Y0), (Z0, X1), (Y1, Z1)), ((X1, Z0), (Y0, Z1), (X0, Y1)))


def gray(place):
    return place ^ (place >> 1)


def label_of(device):
    freq, scan = device % 4, device // 4
    core, y, z = scan % 2, scan // 2 % 4, scan // 8
    return (gray(z) << 4) | (gray(y) << 2) | gray(freq), core


def device_of(label, core):
    x, y, z = gray(label & 3), gray(label >> 2 & 3), gray(label >> 4)
    return ((z * 4 + y) * 2 + core) * 4 + x


def flip(core, stage, step):
    low, high = STAGES[core][stage]
    return (step & 1) * low | (step >> 1) * high


def partners(stage, step):
    pairs = []
    for device in range(128):
        label, core = label_of(device)
        pairs.append((device, device_of(label ^ flip(core, stage, step), core)))
    return pairs


def turn(steps):
    quarter = (steps + 128) >> 8
    x = (steps - quarter * 256).astype(jnp.float32) * (2.0 * math.pi / 1024)
    x2 = x * x
    sine = x * (1 + x2 * (-1 / 6 + x2 * (1 / 120 + x2 * (-1 / 5040 + x2 * (1 / 362880)))))
    cosine = 1 + x2 * (-1 / 2 + x2 * (1 / 24 + x2 * (-1 / 720 + x2 * (1 / 40320 - x2 * (1 / 3628800)))))
    swap, minus_c, minus_s = quarter & 1, (quarter + 1) & 2, quarter & 2
    c, s = jnp.where(swap == 1, sine, cosine), jnp.where(swap == 1, cosine, sine)
    return jnp.where(minus_c == 2, -c, c), jnp.where(minus_s == 2, -s, s)


def halves(value):
    high = value.astype(jnp.bfloat16)
    return high, (value - high.astype(jnp.float32)).astype(jnp.bfloat16)


def dot(left, right):
    return jnp.dot(left, right, preferred_element_type=jnp.float32)


def iota(shape, dim):
    return lax.broadcasted_iota(jnp.int32, shape, dim)


def one_hot(hit):
    return jnp.where(hit, 1.0, 0.0).astype(jnp.bfloat16)


def place_of(core, label):
    x, y, z = gray(label & 3), gray(label >> 2 & 3), gray(label >> 4)
    return ((z * 4 + y) * 2 + core) * 4 + x


def fill_matrix(wc, ws, ct, st, high, low):
    tiles = wc.shape[0]
    c, s = ct.reshape(tiles, 8, 128), st.reshape(tiles, 8, 128)
    for at in range(0, wc.shape[1], 128):
        a, b = wc[:, at : at + 128][:, None, :], ws[:, at : at + 128][:, None, :]
        both = jnp.concatenate([a * c - b * s, -(a * s + b * c)], axis=1)
        high[:, at : at + 128], low[:, at : at + 128] = halves(both.reshape(tiles * 16, 128))


def product(a_high, a_low, f_high, f_low):
    return dot(a_high[...], f_high[...]) + dot(a_low[...], f_high[...]) + dot(a_high[...], f_low[...])


def own_kernel(where, frames, masks, aperture, phases, part, wc, ws, ct2, st2, ct, st, a_high, a_low, f_high, f_low):
    scan, freq = where[0], where[1]
    core, y, z = scan & 1, scan >> 1 & 3, scan >> 3
    label = (gray(z) << 4) | (gray(y) << 2) | gray(freq)
    index = iota((64, 128), 0)
    flips = 0
    for stage in range(3):
        for low in range(2):
            bit = jnp.where(core == 0, STAGES[0][stage][low], STAGES[1][stage][low])
            flips = flips + (index >> (4 - 2 * stage + low) & 1) * bit
    tile = place_of(core, label ^ flips)
    lane_pixel = freq * 32 + (iota((128, 1024), 1) >> 5)
    spread = one_hot(iota((128, 1024), 0) == lane_pixel)
    chosen = one_hot(tile == iota((64, 128), 1))
    mask = dot(chosen, masks[...].astype(jnp.float32).astype(jnp.bfloat16)).astype(jnp.bfloat16)
    mask = dot(mask, spread)
    entry = jnp.broadcast_to(aperture[...].astype(jnp.float32), (8, 128)).astype(jnp.bfloat16)
    entry = dot(entry, spread)[:1].astype(jnp.int32)
    pick = one_hot(iota((256, 1024), 0) == entry)
    turns = phases[...]
    parts = []
    for value in (jnp.cos(turns), jnp.sin(turns)):
        for _ in range(3):
            piece = value.astype(jnp.bfloat16).astype(jnp.float32)
            parts.append(piece)
            value = value - piece
    parts = jnp.concatenate(parts + parts[:2], axis=0).astype(jnp.bfloat16)
    picked = dot(parts, pick)
    wc[...] = mask * (picked[0:1] + picked[1:2] + picked[2:3])
    ws[...] = mask * (picked[3:4] + picked[4:5] + picked[5:6])
    for rows, c_out, s_out in ((scan, ct, st), (scan ^ 1, ct2, st2)):
        row = rows * 32 + (iota((64, 128), 1) & 31)
        c1, s1 = turn(tile * 8 * row & 1023)
        row = rows * 32 + (iota((8, 128), 1) & 31)
        c2, s2 = turn(iota((8, 128), 0) * row & 1023)
        c1, s1 = c1[:, None, :], s1[:, None, :]
        c_out[...] = (c1 * c2[None] - s1 * s2[None]).reshape(512, 128)
        s_out[...] = (s1 * c2[None] + c1 * s2[None]).reshape(512, 128)
    f_high[...], f_low[...] = halves(frames[...])

    @pl.loop(0, 4)
    def _(step):
        tiles, rows = pl.ds(pl.multiple_of(step * 16, 16), 16), pl.ds(pl.multiple_of(step * 128, 128), 128)
        fill_matrix(wc[tiles, :], ws[tiles, :], ct[rows, :], st[rows, :], a_high, a_low)
        part[pl.ds(pl.multiple_of(step * 256, 256), 256), :] = product(a_high, a_low, f_high, f_low)


def other_kernel(step, split, frames, part, wc, ws, ct, st, *refs):
    if split:
        out, f_high, f_low, a_high, a_low = refs
        f_high[...], f_low[...] = halves(frames[0][...])
    else:
        out, a_high, a_low = refs
        f_high, f_low = frames
    tiles, rows = slice(step * 16, step * 16 + 16), slice(step * 128, step * 128 + 128)
    fill_matrix(wc[tiles, :], ws[tiles, :], ct[rows, :], st[rows, :], a_high, a_low)
    out[...] = part[step * 256 : step * 256 + 256, :] + product(a_high, a_low, f_high, f_low)


def sum_kernel(a, b, c, d, *outs):
    rows = outs[0].shape[0]
    for step, out in enumerate(outs):
        at = slice(step * rows, step * rows + rows)
        out[...] = a[at, :] + b[at, :] + c[at, :] + d[at, :]


def last_kernel(a, b, c, d, t_high, t_low, out):
    total = a[...] + b[...] + c[...] + d[...]
    columns = total.shape[1]
    high, low = halves(total)
    both = dot(jnp.concatenate([high, low], axis=0), t_high[...])
    both = both[:16] + both[16:] + dot(high, t_low[...])
    out[:, 0, :] = both[:8, :columns] + both[8:, columns:]
    out[:, 1, :] = both[8:, :columns] - both[:8, columns:]


def call(kernel, outs, scratch=(), flops=0, moved=0, inputs=0, limit=40 << 20):
    one = not isinstance(outs, (list, tuple))
    return pl.pallas_call(
        kernel,
        out_shape=outs,
        in_specs=[pl.BlockSpec(memory_space=pltpu.VMEM)] * inputs,
        out_specs=pl.BlockSpec(memory_space=pltpu.VMEM) if one else [pl.BlockSpec(memory_space=pltpu.VMEM)] * len(outs),
        scratch_shapes=list(scratch),
        cost_estimate=pl.CostEstimate(flops=flops, bytes_accessed=moved, transcendentals=0),
        compiler_params=pltpu.CompilerParams(vmem_limit_bytes=limit),
    )


def f32(*shape):
    return jax.ShapeDtypeStruct(shape, jnp.float32)


def bf16(*shape):
    return jax.ShapeDtypeStruct(shape, jnp.bfloat16)


def body(frames, intersection_masks, aperture, phases):
    col_len = frames.shape[2]
    where = jnp.stack([lax.axis_index("scan"), lax.axis_index("freq")]).astype(jnp.int32)
    swap = [(d, (d // 4 ^ 1) * 4 + d % 4) for d in range(128)]
    other = lax.ppermute(frames, AXES, swap).reshape(1024, col_len)
    vmem = pl.BlockSpec(memory_space=pltpu.VMEM)
    part, wc, ws, ct, st = pl.pallas_call(
        own_kernel,
        out_shape=[f32(1024, col_len), f32(64, 1024), f32(64, 1024), f32(512, 128), f32(512, 128)],
        in_specs=[pl.BlockSpec(memory_space=pltpu.SMEM)] + [vmem] * 4,
        out_specs=[vmem] * 5,
        scratch_shapes=[pltpu.VMEM((512, 128), jnp.float32)] * 2
        + [pltpu.VMEM((256, 1024), jnp.bfloat16)] * 2
        + [pltpu.VMEM((1024, col_len), jnp.bfloat16)] * 2,
        cost_estimate=pl.CostEstimate(flops=6 * 1024 * 1024 * 512, bytes_accessed=5 << 20, transcendentals=0),
        compiler_params=pltpu.CompilerParams(vmem_limit_bytes=24 << 20),
    )(where, frames.reshape(1024, col_len), intersection_masks, aperture[None, :], phases[None, :])

    a_scratch = [pltpu.VMEM((256, 1024), jnp.bfloat16)] * 2
    cost = dict(flops=6 * 256 * 1024 * 512, moved=4 << 20)

    def first(step, split, *given):
        outs = [f32(256, col_len)] + ([bf16(1024, col_len)] * 2 if split else [])
        count = len(given)

        def kernel(*refs):
            other_kernel(step, split, refs[:count], *refs[count:])

        return call(kernel, outs, a_scratch, inputs=count + 5, limit=24 << 20, **cost)(*given, part, wc, ws, ct, st)

    send = {}
    send[3], f_high, f_low = first(3, True, other)
    for step in (1, 2, 0):
        (send[step],) = first(step, False, f_high, f_low)
    columns = np.arange(col_len)
    angle = 2.0 * np.pi / col_len * (columns[:, None] * columns[None, :] % col_len)
    scale = 1.0 / math.sqrt(1024 * col_len * 128)
    table = np.concatenate([np.cos(angle), np.sin(angle)], 1) * scale
    t_high = table.astype(jnp.bfloat16)
    t_low = (table - t_high.astype(np.float64)).astype(jnp.bfloat16)
    for stage in range(3):
        got = [lax.ppermute(send[step], AXES, partners(stage, step)) for step in (3, 1, 2)]
        if stage < 2:
            rows = got[0].shape[0] // 4
            send = call(sum_kernel, [f32(rows, col_len)] * 4, inputs=4, moved=rows << 15, limit=8 << 20)(send[0], *got)
    return call(last_kernel, f32(8, 2, col_len), inputs=6, flops=1 << 26, moved=2 << 20, limit=8 << 20)(
        send[0], *got, jnp.asarray(t_high), jnp.asarray(t_low)
    )


def solution(mesh):
    in_specs = (P("freq", "scan", None), P(), P(), P())
    out_specs = P(("scan", "freq"), None, None)
    return jax.shard_map(body, mesh=mesh, in_specs=in_specs, out_specs=out_specs, check_vma=False)
```

profile of v0, /device:TPU:0, one launch (start us, length us, event | category | flops | bytes accessed | tf_op | source)
XLA Modules:
  0.0 53.9 jit_solution(9681210968577141640)
XLA Ops:
  0.0 0.0 collective-permute-start
  0.0 0.1 pad_add_fusion.where
  0.1 0.0 copy-start.2
  0.1 1.6 %copy-done.2 = f32[32,32,512]{2,1,0:T(8,128)S(1)} copy-done((f32[32,32,512]{2,1,0:T(8,128)S(1)}, f32[32,32,512]{2,1,0:T(8,128)}, u32[]{:S(2)}) %copy-start.2) | copy-done | bytes 2097176
  1.7 0.0 copy-start.3
  1.7 0.8 %copy-done.3 = s32[128,128]{1,0:T(8,128)S(1)} copy-done((s32[128,128]{1,0:T(8,128)S(1)}, s32[128,128]{1,0:T(8,128)}, u32[]{:S(2)}) %copy-start.3) | copy-done | bytes 65560
  2.5 0.0 copy-start.4
  2.5 0.7 %copy-done.4 = f32[256]{0:T(256)S(1)} copy-done((f32[256]{0:T(256)S(1)}, f32[256]{0:T(256)}, u32[]{:S(2)}) %copy-start.4) | copy-done | bytes 1048
  3.2 0.0 copy-start.5
  3.2 0.7 %copy-done.5 = s32[128]{0:T(128)S(1)} copy-done((s32[128]{0:T(128)S(1)}, s32[128]{0:T(128)}, u32[]{:S(2)}) %copy-start.5) | copy-done | bytes 536
  3.8 6.6 %shard_map.64 = (f32[1024,512]{1,0:T(8,128)S(1)}, f32[64,1024]{1,0:T(8,128)S(1)}, f32[64,1024]{1,0:T(8,128)S(1)}, f32[512,128]{1,0:T(8,128)S(1)}, f32[512,128]{1,0:T(8,128)S(1)}) custom-call(s32[2]{0:T(128)S(1)} %pad_add_fusion.where, f32[1024,512]{1,0:T(8,128)S(1)} %bitcast.7, s32[128,128]{1,0:T(8,128)S(1)} %copy-done.3, s32[1,128]{1,0:T(1,128)S(1)} %bitcast.9, ...), custom_call_target="tpu_custom_call" | custom-call | flops 3221225472 | bytes 5242880 | tf_op jit(solution)/shard_map/pallas_call | solution.py:193
  10.5 0.0 collective-permute-done
  10.5 1.3 %shard_map.65 = (f32[256,512]{1,0:T(8,128)S(1)}, bf16[1024,512]{1,0:T(8,128)(2,1)S(1)}, bf16[1024,512]{1,0:T(8,128)(2,1)S(1)}) custom-call(f32[1024,512]{1,0:T(8,128)S(1)} %bitcast.6, f32[1024,512]{1,0:T(8,128)S(1)} %get-tuple-element.21.refs_1_.refs_2_, f32[64,1024]{1,0:T(8,128)S(1)} %get-tuple-element.22.refs_2_.refs_3_, ...), custom_call_target="tpu_custom_call" | custom-call | flops 805306368 | bytes 4194304 | tf_op jit(solution)/shard_map/pallas_call | solution.py:215
  11.9 1.2 %shard_map.68 = f32[256,512]{1,0:T(8,128)S(1)} custom-call(bf16[1024,512]{1,0:T(8,128)(2,1)S(1)} %get-tuple-element.26.refs_0_, bf16[1024,512]{1,0:T(8,128)(2,1)S(1)} %get-tuple-element.27.refs_1_, f32[1024,512]{1,0:T(8,128)S(1)} %get-tuple-element.21.refs_1_.refs_2_, f32[64,1024]{1,0:T(8,128)S(1)} %get-tuple-element.22.refs_2_.refs_3_, ...), custom_call_target="tpu_custom_call" | custom-call | flops 805306368 | bytes 4194304 | tf_op jit(solution)/shard_map/pallas_call | solution.py:215
  13.1 1.2 %shard_map.67 = f32[256,512]{1,0:T(8,128)S(1)} custom-call(bf16[1024,512]{1,0:T(8,128)(2,1)S(1)} %get-tuple-element.26.refs_0_, bf16[1024,512]{1,0:T(8,128)(2,1)S(1)} %get-tuple-element.27.refs_1_, f32[1024,512]{1,0:T(8,128)S(1)} %get-tuple-element.21.refs_1_.refs_2_, f32[64,1024]{1,0:T(8,128)S(1)} %get-tuple-element.22.refs_2_.refs_3_, ...), custom_call_target="tpu_custom_call" | custom-call | flops 805306368 | bytes 4194304 | tf_op jit(solution)/shard_map/pallas_call | solution.py:215
  14.3 1.7 %collective-permute-start.2 = (f32[256,512]{1,0:T(8,128)S(1)}, f32[256,512]{1,0:T(8,128)S(1)}, u32[]{:S(2)}, u32[]{:S(2)}) collective-permute-start(f32[256,512]{1,0:T(8,128)S(1)} %shard_map.67), channel_id=1, source_target_pairs={{0,1},{1,0},{2,3},{3,2},{4,7},{5,6},{6,5},{7,4},{8,9},{9,8},{10,11... | collective-permute-start | bytes 1572872 | tf_op jit(solution)/shard_map/ppermute | solution.py:228
  16.0 1.6 %collective-permute-start.3 = (f32[256,512]{1,0:T(8,128)S(1)}, f32[256,512]{1,0:T(8,128)S(1)}, u32[]{:S(2)}, u32[]{:S(2)}) collective-permute-start(f32[256,512]{1,0:T(8,128)S(1)} %shard_map.68), channel_id=1, source_target_pairs={{0,8},{1,9},{2,10},{3,11},{4,36},{5,37},{6,38},{7,39},{8,0},{9,1},... | collective-permute-start | bytes 1572872 | tf_op jit(solution)/shard_map/ppermute | solution.py:228
  17.5 0.3 collective-permute-start.1
  17.9 1.2 %shard_map.66.a = f32[256,512]{1,0:T(8,128)S(1)} custom-call(bf16[1024,512]{1,0:T(8,128)(2,1)S(1)} %get-tuple-element.26.refs_0_, bf16[1024,512]{1,0:T(8,128)(2,1)S(1)} %get-tuple-element.27.refs_1_, f32[1024,512]{1,0:T(8,128)S(1)} %get-tuple-element.21.refs_1_.refs_2_, f32[64,1024]{1,0:T(8,128)S(1)} %get-tuple-element.22.refs_2_.refs_3_, ...), custom_call_target="tpu_custom_call" | custom-call | flops 805306368 | bytes 4194304 | tf_op jit(solution)/shard_map/pallas_call | solution.py:215
  19.1 0.0 copy-start
  19.1 0.0 copy-start.1
  19.1 4.4 %collective-permute-done.2.c = f32[256,512]{1,0:T(8,128)S(1)} collective-permute-done((f32[256,512]{1,0:T(8,128)S(1)}, f32[256,512]{1,0:T(8,128)S(1)}, u32[]{:S(2)}, u32[]{:S(2)}) %collective-permute-start.2) | collective-permute-done | bytes 524320 | tf_op jit(solution)/shard_map/ppermute | solution.py:228
  23.6 7.2 %collective-permute-done.3.d = f32[256,512]{1,0:T(8,128)S(1)} collective-permute-done((f32[256,512]{1,0:T(8,128)S(1)}, f32[256,512]{1,0:T(8,128)S(1)}, u32[]{:S(2)}, u32[]{:S(2)}) %collective-permute-start.3) | collective-permute-done | bytes 524320 | tf_op jit(solution)/shard_map/ppermute | solution.py:228
  30.8 0.0 collective-permute-done.1.b
  30.8 0.1 shard_map.69
  30.9 3.7 %collective-permute-start.4 = (f32[64,512]{1,0:T(8,128)S(1)}, f32[64,512]{1,0:T(8,128)S(1)}, u32[]{:S(2)}, u32[]{:S(2)}) collective-permute-start(f32[64,512]{1,0:T(8,128)S(1)} %get-tuple-element.30), channel_id=1, source_target_pairs={{0,35},{1,34},{2,33},{3,32},{4,108},{5,109},{6,110},{7,111},{8,43}... | collective-permute-start | bytes 393224 | tf_op jit(solution)/shard_map/ppermute | solution.py:228
  34.6 0.1 collective-permute-start.5
  34.7 0.9 %collective-permute-start.6 = (f32[64,512]{1,0:T(8,128)S(1)}, f32[64,512]{1,0:T(8,128)S(1)}, u32[]{:S(2)}, u32[]{:S(2)}) collective-permute-start(f32[64,512]{1,0:T(8,128)S(1)} %get-tuple-element.32), channel_id=1, source_target_pairs={{0,3},{1,2},{2,1},{3,0},{4,100},{5,101},{6,102},{7,103},{8,11},{9,... | collective-permute-start | bytes 393224 | tf_op jit(solution)/shard_map/ppermute | solution.py:228
  35.6 2.4 %collective-permute-done.4.b = f32[64,512]{1,0:T(8,128)S(1)} collective-permute-done((f32[64,512]{1,0:T(8,128)S(1)}, f32[64,512]{1,0:T(8,128)S(1)}, u32[]{:S(2)}, u32[]{:S(2)}) %collective-permute-start.4) | collective-permute-done | bytes 131104 | tf_op jit(solution)/shard_map/ppermute | solution.py:228
  38.0 1.5 %collective-permute-done.5.c = f32[64,512]{1,0:T(8,128)S(1)} collective-permute-done((f32[64,512]{1,0:T(8,128)S(1)}, f32[64,512]{1,0:T(8,128)S(1)}, u32[]{:S(2)}, u32[]{:S(2)}) %collective-permute-start.5) | collective-permute-done | bytes 131104 | tf_op jit(solution)/shard_map/ppermute | solution.py:228
  39.5 1.3 %collective-permute-done.6.d = f32[64,512]{1,0:T(8,128)S(1)} collective-permute-done((f32[64,512]{1,0:T(8,128)S(1)}, f32[64,512]{1,0:T(8,128)S(1)}, u32[]{:S(2)}, u32[]{:S(2)}) %collective-permute-start.6) | collective-permute-done | bytes 131104 | tf_op jit(solution)/shard_map/ppermute | solution.py:228
  40.9 6.4 %collective-permute-start.7 = (f32[16,512]{1,0:T(8,128)S(1)}, f32[16,512]{1,0:T(8,128)S(1)}, u32[]{:S(2)}, u32[]{:S(2)}) collective-permute-start(f32[16,512]{1,0:T(8,128)S(1)} %get-tuple-element.34), channel_id=1, source_target_pairs={{0,120},{1,121},{2,122},{3,123},{4,29},{5,28},{6,31},{7,30},{8,112... | collective-permute-start | bytes 98312 | tf_op jit(solution)/shard_map/ppermute | solution.py:228
  47.3 0.4 collective-permute-start.8
  47.7 0.3 collective-permute-start.9
  47.9 1.2 %collective-permute-done.7.b = f32[16,512]{1,0:T(8,128)S(1)} collective-permute-done((f32[16,512]{1,0:T(8,128)S(1)}, f32[16,512]{1,0:T(8,128)S(1)}, u32[]{:S(2)}, u32[]{:S(2)}) %collective-permute-start.7) | collective-permute-done | bytes 32800 | tf_op jit(solution)/shard_map/ppermute | solution.py:228
  49.2 3.2 %collective-permute-done.8.c = f32[16,512]{1,0:T(8,128)S(1)} collective-permute-done((f32[16,512]{1,0:T(8,128)S(1)}, f32[16,512]{1,0:T(8,128)S(1)}, u32[]{:S(2)}, u32[]{:S(2)}) %collective-permute-start.8) | collective-permute-done | bytes 32800 | tf_op jit(solution)/shard_map/ppermute | solution.py:228
  52.4 0.4 collective-permute-done.9.d
  52.8 0.0 copy-done
  52.8 0.0 copy-done.1
  52.8 1.0 %shard_map.71 = f32[8,2,512]{2,1,0:T(2,128)} custom-call(f32[16,512]{1,0:T(8,128)S(1)} %get-tuple-element.33.a, f32[16,512]{1,0:T(8,128)S(1)} %collective-permute-done.7.b, f32[16,512]{1,0:T(8,128)S(1)} %collective-permute-done.8.c, f32[16,512]{1,0:T(8,128)S(1)} %collective-permute-done.9.d, bf16[512,1024]{1,0:T(8,128)(2,1)S(1)} %copy-done.1, ...), custom_call_target="tpu_custom_call" | custom-call | flops 67108864 | bytes 2097152 | tf_op jit(solution)/shard_map/pallas_call | solution.py:232
  (1 shorter events, 0.0 us)
Async XLA Ops:
  0.0 10.5 %collective-permute-start = (f32[32,32,512]{2,1,0:T(8,128)}, f32[32,32,512]{2,1,0:T(8,128)S(1)}, u32[]{:S(2)}, u32[]{:S(2)}) collective-permute-start(f32[32,32,512]{2,1,0:T(8,128)} %param.6), channel_id=1, source_target_pairs={{0,4},{1,5},{2,6},{3,7},{4,0},{5,1},{6,2},{7,3},{8,12},{9,13},{10,... | collective-permute-start | bytes 6291464 | tf_op jit(solution)/shard_map/ppermute | solution.py:191
  0.1 1.6 %copy-start.2 = (f32[32,32,512]{2,1,0:T(8,128)S(1)}, f32[32,32,512]{2,1,0:T(8,128)}, u32[]{:S(2)}) copy-start(f32[32,32,512]{2,1,0:T(8,128)} %param.6) | copy-start | bytes 6291460
  1.7 0.8 %copy-start.3 = (s32[128,128]{1,0:T(8,128)S(1)}, s32[128,128]{1,0:T(8,128)}, u32[]{:S(2)}) copy-start(s32[128,128]{1,0:T(8,128)} %masks.1) | copy-start | bytes 196612
  2.5 0.7 %copy-start.4 = (f32[256]{0:T(256)S(1)}, f32[256]{0:T(256)}, u32[]{:S(2)}) copy-start(f32[256]{0:T(256)} %param.9) | copy-start | bytes 3076
  3.2 0.7 %copy-start.5 = (s32[128]{0:T(128)S(1)}, s32[128]{0:T(128)}, u32[]{:S(2)}) copy-start(s32[128]{0:T(128)} %param.8) | copy-start | bytes 1540
  14.3 9.3 %collective-permute-start.2 = (f32[256,512]{1,0:T(8,128)S(1)}, f32[256,512]{1,0:T(8,128)S(1)}, u32[]{:S(2)}, u32[]{:S(2)}) collective-permute-start(f32[256,512]{1,0:T(8,128)S(1)} %shard_map.67), channel_id=1, source_target_pairs={{0,1},{1,0},{2,3},{3,2},{4,7},{5,6},{6,5},{7,4},{8,9},{9,8},{10,11... | collective-permute-start | bytes 1572872 | tf_op jit(solution)/shard_map/ppermute | solution.py:228
  16.0 14.8 %collective-permute-start.3 = (f32[256,512]{1,0:T(8,128)S(1)}, f32[256,512]{1,0:T(8,128)S(1)}, u32[]{:S(2)}, u32[]{:S(2)}) collective-permute-start(f32[256,512]{1,0:T(8,128)S(1)} %shard_map.68), channel_id=1, source_target_pairs={{0,8},{1,9},{2,10},{3,11},{4,36},{5,37},{6,38},{7,39},{8,0},{9,1},... | collective-permute-start | bytes 1572872 | tf_op jit(solution)/shard_map/ppermute | solution.py:228
  17.5 13.2 %collective-permute-start.1 = (f32[256,512]{1,0:T(8,128)S(1)}, f32[256,512]{1,0:T(8,128)S(1)}, u32[]{:S(2)}, u32[]{:S(2)}) collective-permute-start(f32[256,512]{1,0:T(8,128)S(1)} %get-tuple-element.28), channel_id=1, source_target_pairs={{0,9},{1,8},{2,11},{3,10},{4,39},{5,38},{6,37},{7,36},{8,1},{9,0},... | collective-permute-start | bytes 1572872 | tf_op jit(solution)/shard_map/ppermute | solution.py:228
  19.1 33.7 %copy-start = (bf16[512,1024]{1,0:T(8,128)(2,1)S(1)}, bf16[512,1024]{1,0:T(8,128)(2,1)}, u32[]{:S(2)}) copy-start(bf16[512,1024]{1,0:T(8,128)(2,1)} %constant.14.clone.t_low) | copy-start | bytes 3145732
  19.1 33.7 %copy-start.1 = (bf16[512,1024]{1,0:T(8,128)(2,1)S(1)}, bf16[512,1024]{1,0:T(8,128)(2,1)}, u32[]{:S(2)}) copy-start(bf16[512,1024]{1,0:T(8,128)(2,1)} %constant.13.clone.t_high) | copy-start | bytes 3145732
  30.9 7.2 %collective-permute-start.4 = (f32[64,512]{1,0:T(8,128)S(1)}, f32[64,512]{1,0:T(8,128)S(1)}, u32[]{:S(2)}, u32[]{:S(2)}) collective-permute-start(f32[64,512]{1,0:T(8,128)S(1)} %get-tuple-element.30), channel_id=1, source_target_pairs={{0,35},{1,34},{2,33},{3,32},{4,108},{5,109},{6,110},{7,111},{8,43}... | collective-permute-start | bytes 393224 | tf_op jit(solution)/shard_map/ppermute | solution.py:228
  34.6 5.0 %collective-permute-start.5 = (f32[64,512]{1,0:T(8,128)S(1)}, f32[64,512]{1,0:T(8,128)S(1)}, u32[]{:S(2)}, u32[]{:S(2)}) collective-permute-start(f32[64,512]{1,0:T(8,128)S(1)} %get-tuple-element.31), channel_id=1, source_target_pairs={{0,32},{1,33},{2,34},{3,35},{4,12},{5,13},{6,14},{7,15},{8,40},{9,... | collective-permute-start | bytes 393224 | tf_op jit(solution)/shard_map/ppermute | solution.py:228
  34.7 6.2 %collective-permute-start.6 = (f32[64,512]{1,0:T(8,128)S(1)}, f32[64,512]{1,0:T(8,128)S(1)}, u32[]{:S(2)}, u32[]{:S(2)}) collective-permute-start(f32[64,512]{1,0:T(8,128)S(1)} %get-tuple-element.32), channel_id=1, source_target_pairs={{0,3},{1,2},{2,1},{3,0},{4,100},{5,101},{6,102},{7,103},{8,11},{9,... | collective-permute-start | bytes 393224 | tf_op jit(solution)/shard_map/ppermute | solution.py:228
  40.9 8.3 %collective-permute-start.7 = (f32[16,512]{1,0:T(8,128)S(1)}, f32[16,512]{1,0:T(8,128)S(1)}, u32[]{:S(2)}, u32[]{:S(2)}) collective-permute-start(f32[16,512]{1,0:T(8,128)S(1)} %get-tuple-element.34), channel_id=1, source_target_pairs={{0,120},{1,121},{2,122},{3,123},{4,29},{5,28},{6,31},{7,30},{8,112... | collective-permute-start | bytes 98312 | tf_op jit(solution)/shard_map/ppermute | solution.py:228
  47.3 5.1 %collective-permute-start.8 = (f32[16,512]{1,0:T(8,128)S(1)}, f32[16,512]{1,0:T(8,128)S(1)}, u32[]{:S(2)}, u32[]{:S(2)}) collective-permute-start(f32[16,512]{1,0:T(8,128)S(1)} %get-tuple-element.35), channel_id=1, source_target_pairs={{0,24},{1,25},{2,26},{3,27},{4,5},{5,4},{6,7},{7,6},{8,16},{9,17},... | collective-permute-start | bytes 98312 | tf_op jit(solution)/shard_map/ppermute | solution.py:228
  47.7 5.1 %collective-permute-start.9 = (f32[16,512]{1,0:T(8,128)S(1)}, f32[16,512]{1,0:T(8,128)S(1)}, u32[]{:S(2)}, u32[]{:S(2)}) collective-permute-start(f32[16,512]{1,0:T(8,128)S(1)} %get-tuple-element.36), channel_id=1, source_target_pairs={{0,96},{1,97},{2,98},{3,99},{4,28},{5,29},{6,30},{7,31},{8,104},{9... | collective-permute-start | bytes 98312 | tf_op jit(solution)/shard_map/ppermute | solution.py:228
where the time goes:
time: 54.1 us; the launch traced here: 53.9 us
  waiting for transfers between devices  21.7 us (40%)
  starting transfers between devices  15.4 us (28%)
  Pallas kernels  12.8 us (24%)
  local copies, waits for them, and re-layouts  3.78 us (7%)
    ppermute x9, waiting for transfers between devices, body(): lax.ppermute(send[step], AXES, partners(stage, step))  21.7 us
    ppermute x9, starting transfers between devices, body(): lax.ppermute(send[step], AXES, partners(stage, step))  15.4 us
    pallas_call x1, Pallas kernels, body(): pl.pallas_call(own_kernel, out_shape=[f32(1024, col_len), f32(64, 1024),...  6.64 us
    pallas_call x4, Pallas kernels, first(): call(kernel, outs, a_scratch, inputs=count + 5, limit=24 << 20, **cost)  4.99 us
    unnamed x12, local copies, waits for them, and re-layouts  3.78 us
  transfers between devices with their start and end apart: 10, of which 8 were waited for; matrix products, arithmetic and copies ran while one was open for 0% of the time, Pallas kernels for 15%

commit v1 on v0

--- a/solution.py
+++ b/solution.py
@@ -1,3 +1,4 @@
+import functools
 import math
 
 import jax
@@ -87,7 +88,18 @@
     return dot(a_high[...], f_high[...]) + dot(a_low[...], f_high[...]) + dot(a_high[...], f_low[...])
 
 
-def own_kernel(where, frames, masks, aperture, phases, part, wc, ws, ct2, st2, ct, st, a_high, a_low, f_high, f_low):
+def own_kernel(
+    where, frames_in, masks_in, aperture_in, phases_in, part, wc, ws, ct, st, ct2, st2, f_high, f_low,
+    frames, masks, aperture, phases, a_high, a_low, sems,
+):
+    copies = [
+        pltpu.make_async_copy(src, dst, sems.at[at])
+        for at, (src, dst) in enumerate(
+            ((frames_in, frames), (masks_in, masks), (aperture_in, aperture), (phases_in, phases))
+        )
+    ]
+    for copy in copies[1:] + copies[:1]:
+        copy.start()
     scan, freq = where[0], where[1]
     core, y, z = scan & 1, scan >> 1 & 3, scan >> 3
     label = (gray(z) << 4) | (gray(y) << 2) | gray(freq)
@@ -101,6 +113,8 @@
     lane_pixel = freq * 32 + (iota((128, 1024), 1) >> 5)
     spread = one_hot(iota((128, 1024), 0) == lane_pixel)
     chosen = one_hot(tile == iota((64, 128), 1))
+    for copy in copies[1:]:
+        copy.wait()
     mask = dot(chosen, masks[...].astype(jnp.float32).astype(jnp.bfloat16)).astype(jnp.bfloat16)
     mask = dot(mask, spread)
     entry = jnp.broadcast_to(aperture[...].astype(jnp.float32), (8, 128)).astype(jnp.bfloat16)
@@ -125,25 +139,40 @@
         c1, s1 = c1[:, None, :], s1[:, None, :]
         c_out[...] = (c1 * c2[None] - s1 * s2[None]).reshape(512, 128)
         s_out[...] = (s1 * c2[None] + c1 * s2[None]).reshape(512, 128)
+    copies[0].wait()
     f_high[...], f_low[...] = halves(frames[...])
 
-    @pl.loop(0, 4)
+    @pl.loop(1, 4)
     def _(step):
         tiles, rows = pl.ds(pl.multiple_of(step * 16, 16), 16), pl.ds(pl.multiple_of(step * 128, 128), 128)
         fill_matrix(wc[tiles, :], ws[tiles, :], ct[rows, :], st[rows, :], a_high, a_low)
         part[pl.ds(pl.multiple_of(step * 256, 256), 256), :] = product(a_high, a_low, f_high, f_low)
 
 
-def other_kernel(step, split, frames, part, wc, ws, ct, st, *refs):
-    if split:
-        out, f_high, f_low, a_high, a_low = refs
-        f_high[...], f_low[...] = halves(frames[0][...])
-    else:
-        out, a_high, a_low = refs
-        f_high, f_low = frames
+def later_kernel(step, frames, part, wc, ws, ct, st, out, a_high, a_low, f_high, f_low):
+    f_high[...], f_low[...] = halves(frames[...])
     tiles, rows = slice(step * 16, step * 16 + 16), slice(step * 128, step * 128 + 128)
     fill_matrix(wc[tiles, :], ws[tiles, :], ct[rows, :], st[rows, :], a_high, a_low)
     out[...] = part[step * 256 : step * 256 + 256, :] + product(a_high, a_low, f_high, f_low)
+
+
+def near_kernel(own_high, own_low, frames, wc, ws, ct, st, ct2, st2, out, a_high, a_low, f_high, f_low):
+    fill_matrix(wc[:16, :], ws[:16, :], ct[:128, :], st[:128, :], a_high, a_low)
+    out[...] = product(a_high, a_low, own_high, own_low)
+    f_high[...], f_low[...] = halves(frames[...])
+    fill_matrix(wc[:16, :], ws[:16, :], ct2[:128, :], st2[:128, :], a_high, a_low)
+    out[...] += product(a_high, a_low, f_high, f_low)
+
+
+def add_kernel(a, b, out):
+    out[...] = a[...] + b[...]
+
+
+def split_kernel(a, b, *outs):
+    rows = outs[0].shape[0]
+    for step, out in enumerate(outs):
+        at = slice(step * rows, step * rows + rows)
+        out[...] = a[at, :] + b[at, :]
 
 
 def sum_kernel(a, b, c, d, *outs):
@@ -190,45 +219,45 @@
     swap = [(d, (d // 4 ^ 1) * 4 + d % 4) for d in range(128)]
     other = lax.ppermute(frames, AXES, swap).reshape(1024, col_len)
     vmem = pl.BlockSpec(memory_space=pltpu.VMEM)
-    part, wc, ws, ct, st = pl.pallas_call(
+    part, wc, ws, ct, st, ct2, st2, f_high, f_low = pl.pallas_call(
         own_kernel,
-        out_shape=[f32(1024, col_len), f32(64, 1024), f32(64, 1024), f32(512, 128), f32(512, 128)],
-        in_specs=[pl.BlockSpec(memory_space=pltpu.SMEM)] + [vmem] * 4,
-        out_specs=[vmem] * 5,
-        scratch_shapes=[pltpu.VMEM((512, 128), jnp.float32)] * 2
+        out_shape=[f32(1024, col_len)] + [f32(64, 1024)] * 2 + [f32(512, 128)] * 4 + [bf16(1024, col_len)] * 2,
+        in_specs=[pl.BlockSpec(memory_space=pltpu.SMEM)] + [pl.BlockSpec(memory_space=pltpu.HBM)] * 4,
+        out_specs=[vmem] * 9,
+        scratch_shapes=[
+            pltpu.VMEM((1024, col_len), jnp.float32),
+            pltpu.VMEM((128, 128), jnp.int32),
+            pltpu.VMEM((1, 128), jnp.int32),
+            pltpu.VMEM((1, 256), jnp.float32),
+        ]
         + [pltpu.VMEM((256, 1024), jnp.bfloat16)] * 2
-        + [pltpu.VMEM((1024, col_len), jnp.bfloat16)] * 2,
-        cost_estimate=pl.CostEstimate(flops=6 * 1024 * 1024 * 512, bytes_accessed=5 << 20, transcendentals=0),
+        + [pltpu.SemaphoreType.DMA((4,))],
+        cost_estimate=pl.CostEstimate(flops=6 * 768 * 1024 * 512, bytes_accessed=5 << 20, transcendentals=0),
         compiler_params=pltpu.CompilerParams(vmem_limit_bytes=24 << 20),
-    )(where, frames.reshape(1024, col_len), intersection_masks, aperture[None, :], phases[None, :])
-
-    a_scratch = [pltpu.VMEM((256, 1024), jnp.bfloat16)] * 2
-    cost = dict(flops=6 * 256 * 1024 * 512, moved=4 << 20)
-
-    def first(step, split, *given):
-        outs = [f32(256, col_len)] + ([bf16(1024, col_len)] * 2 if split else [])
-        count = len(given)
-
-        def kernel(*refs):
-            other_kernel(step, split, refs[:count], *refs[count:])
-
-        return call(kernel, outs, a_scratch, inputs=count + 5, limit=24 << 20, **cost)(*given, part, wc, ws, ct, st)
-
-    send = {}
-    send[3], f_high, f_low = first(3, True, other)
-    for step in (1, 2, 0):
-        (send[step],) = first(step, False, f_high, f_low)
+    )(where, *[pltpu.with_memory_space_constraint(u, pltpu.HBM) for u in (frames.reshape(1024, col_len), intersection_masks, aperture[None, :], phases[None, :])])
+
+    scratch = [pltpu.VMEM((256, 1024), jnp.bfloat16)] * 2 + [pltpu.VMEM((1024, col_len), jnp.bfloat16)] * 2
+    cost = dict(flops=1000, moved=1000, limit=24 << 20)
+    block = f32(256, col_len)
+    send = {
+        step: call(functools.partial(later_kernel, step), block, scratch, inputs=6, **cost)(other, part, wc, ws, ct2, st2)
+        for step in (3, 1, 2)
+    }
+    send[0] = call(near_kernel, block, scratch, inputs=9, **cost)(f_high, f_low, other, wc, ws, ct, st, ct2, st2)
     columns = np.arange(col_len)
     angle = 2.0 * np.pi / col_len * (columns[:, None] * columns[None, :] % col_len)
     scale = 1.0 / math.sqrt(1024 * col_len * 128)
     table = np.concatenate([np.cos(angle), np.sin(angle)], 1) * scale
     t_high = table.astype(jnp.bfloat16)
     t_low = (table - t_high.astype(np.float64)).astype(jnp.bfloat16)
-    for stage in range(3):
-        got = [lax.ppermute(send[step], AXES, partners(stage, step)) for step in (3, 1, 2)]
-        if stage < 2:
-            rows = got[0].shape[0] // 4
-            send = call(sum_kernel, [f32(rows, col_len)] * 4, inputs=4, moved=rows << 15, limit=8 << 20)(send[0], *got)
+    for step in (3, 1):
+        got = lax.ppermute(send[step], AXES, partners(0, step))
+        send[0] = call(add_kernel, block, inputs=2, moved=3 << 19, limit=8 << 20)(send[0], got)
+    got = lax.ppermute(send[2], AXES, partners(0, 2))
+    send = call(split_kernel, [f32(64, col_len)] * 4, inputs=2, moved=3 << 19, limit=8 << 20)(send[0], got)
+    got = [lax.ppermute(send[step], AXES, partners(1, step)) for step in (3, 1, 2)]
+    send = call(sum_kernel, [f32(16, col_len)] * 4, inputs=4, moved=5 << 17, limit=8 << 20)(send[0], *got)
+    got = [lax.ppermute(send[step], AXES, partners(2, step)) for step in (3, 1, 2)]
     return call(last_kernel, f32(8, 2, col_len), inputs=6, flops=1 << 26, moved=2 << 20, limit=8 << 20)(
         send[0], *got, jnp.asarray(t_high), jnp.asarray(t_low)
     )

time: 54.1 us -> 47.2 us (0.87)
  waiting for transfers between devices: 21.7 us -> 17.9 us
  local copies, waits for them, and re-layouts: 3.78 us -> 0.01 us
  Pallas kernels: 12.8 us -> 13.4 us
    ppermute x9, waiting for transfers between devices: 21.7 us -> 17.9 us  [the longest x2 7.35 us: body(): got = lax.ppermute(send[step], AXES, partners(0, step))]
    unnamed x12 -> x4, local copies, waits for them, and re-layouts: 3.78 us -> 0.01 us
    pallas_call x7 -> x9, Pallas kernels: 11.7 us -> 12.4 us  [the longest x1 6.14 us: body(): pl.pallas_call(own_kernel, out_shape=[f32(1024, col_len)] + [f32(64, 1024...]
  transfers between devices with their start and end apart: 10 -> 10, of which waited for: 8 -> 8; matrix products, arithmetic and copies ran while one was open for 0% -> 0% of each run, Pallas kernels for 15% -> 24%
where the time goes in v1:
time: 47.2 us; the launch traced here: 47.1 us
  waiting for transfers between devices  17.9 us (38%)
  starting transfers between devices  15.6 us (33%)
  Pallas kernels  13.4 us (28%)
    ppermute x2, waiting for transfers between devices, body(): got = lax.ppermute(send[step], AXES, partners(0, step))  7.35 us
    ppermute x3, starting transfers between devices, body(): lax.ppermute(send[step], AXES, partners(2, step))  6.99 us
    pallas_call x1, Pallas kernels, body(): pl.pallas_call(own_kernel, out_shape=[f32(1024, col_len)] + [f32(64, 1024...  6.14 us
    ppermute x3, waiting for transfers between devices, body(): lax.ppermute(send[step], AXES, partners(1, step))  5.62 us
    ppermute x3, waiting for transfers between devices, body(): lax.ppermute(send[step], AXES, partners(2, step))  4.93 us
    ppermute x3, starting transfers between devices, body(): lax.ppermute(send[step], AXES, partners(1, step))  4.86 us
    pallas_call x3, Pallas kernels, body(): call(functools.partial(later_kernel, step), block, scratch, inputs=6, **c...  3.75 us
    ppermute x2, starting transfers between devices, body(): got = lax.ppermute(send[step], AXES, partners(0, step))  3.27 us
  transfers between devices with their start and end apart: 10, of which 8 were waited for; matrix products, arithmetic and copies ran while one was open for 0% of the time, Pallas kernels for 24%

profile of v1, /device:TPU:0, one launch (start us, length us, event | category | flops | bytes accessed | tf_op | source)
XLA Modules:
  0.0 47.1 jit_solution(11893057587505440914)
XLA Ops:
  0.0 0.0 collective-permute-start
  0.0 0.1 pad_add_fusion.where
  0.1 6.1 %shard_map.64 = (f32[1024,512]{1,0:T(8,128)S(1)}, f32[64,1024]{1,0:T(8,128)S(1)}, f32[64,1024]{1,0:T(8,128)S(1)}, f32[512,128]{1,0:T(8,128)S(1)}, f32[512,128]{1...) custom-call(s32[2]{0:T(128)S(1)} %pad_add_fusion.where, ...), custom_call_target="tpu_custom_call" | custom-call | flops 2415919104 | bytes 5242880 | tf_op jit(solution)/shard_map/pallas_call | solution.py:222
  6.2 0.0 collective-permute-done
  6.2 1.3 %shard_map.66 = f32[256,512]{1,0:T(8,128)S(1)} custom-call(f32[1024,512]{1,0:T(8,128)S(1)} %bitcast.6, f32[1024,512]{1,0:T(8,128)S(1)} %get-tuple-element.30.part, f32[64,1024]{1,0:T(8,128)S(1)} %get-tuple-element.24.wc, f32[64,1024]{1,0:T(8,128)S(1)} %get-tuple-element.25.ws, f32[512,128]{1,0:T(8,128)S(1)} %get-tuple-element.28.ct2.ct, ...), custom_call_target="tpu_custom_call" | custom-call | flops 1000 | bytes 1000 | tf_op jit(solution)/shard_map/pallas_call | solution.py:243
  7.5 2.7 %collective-permute-start.1 = (f32[256,512]{1,0:T(8,128)S(1)}, f32[256,512]{1,0:T(8,128)S(1)}, u32[]{:S(2)}, u32[]{:S(2)}) collective-permute-start(f32[256,512]{1,0:T(8,128)S(1)} %shard_map.66), channel_id=1, source_target_pairs={{0,9},{1,8},{2,11},{3,10},{4,39},{5,38},{6,37},{7,36},{8,1},{9,0},... | collective-permute-start | bytes 1572872 | tf_op jit(solution)/shard_map/ppermute | solution.py:254
  10.2 1.2 %shard_map.68 = f32[256,512]{1,0:T(8,128)S(1)} custom-call(f32[1024,512]{1,0:T(8,128)S(1)} %bitcast.7, f32[1024,512]{1,0:T(8,128)S(1)} %get-tuple-element.30.part, f32[64,1024]{1,0:T(8,128)S(1)} %get-tuple-element.24.wc, f32[64,1024]{1,0:T(8,128)S(1)} %get-tuple-element.25.ws, f32[512,128]{1,0:T(8,128)S(1)} %get-tuple-element.28.ct2.ct, ...), custom_call_target="tpu_custom_call" | custom-call | flops 1000 | bytes 1000 | tf_op jit(solution)/shard_map/pallas_call | solution.py:243
  11.4 0.6 %collective-permute-start.2 = (f32[256,512]{1,0:T(8,128)S(1)}, f32[256,512]{1,0:T(8,128)S(1)}, u32[]{:S(2)}, u32[]{:S(2)}) collective-permute-start(f32[256,512]{1,0:T(8,128)S(1)} %shard_map.68), channel_id=1, source_target_pairs={{0,1},{1,0},{2,3},{3,2},{4,7},{5,6},{6,5},{7,4},{8,9},{9,8},{10,11... | collective-permute-start | bytes 1572872 | tf_op jit(solution)/shard_map/ppermute | solution.py:254
  12.0 1.2 %shard_map.70 = f32[256,512]{1,0:T(8,128)S(1)} custom-call(f32[1024,512]{1,0:T(8,128)S(1)} %bitcast.8, f32[1024,512]{1,0:T(8,128)S(1)} %get-tuple-element.30.part, f32[64,1024]{1,0:T(8,128)S(1)} %get-tuple-element.24.wc, f32[64,1024]{1,0:T(8,128)S(1)} %get-tuple-element.25.ws, f32[512,128]{1,0:T(8,128)S(1)} %get-tuple-element.28.ct2.ct, ...), custom_call_target="tpu_custom_call" | custom-call | flops 1000 | bytes 1000 | tf_op jit(solution)/shard_map/pallas_call | solution.py:243
  13.3 0.5 collective-permute-start.3
  13.7 2.3 %shard_map.65.a = f32[256,512]{1,0:T(8,128)S(1)} custom-call(bf16[1024,512]{1,0:T(8,128)(2,1)S(1)} %get-tuple-element.22.own_high, bf16[1024,512]{1,0:T(8,128)(2,1)S(1)} %get-tuple-element.23.own_low, f32[1024,512]{1,0:T(8,128)S(1)} %bitcast.9, f32[64,1024]{1,0:T(8,128)S(1)} %get-tuple-element.24.wc, f32[64,1024]{1,0:T(8,128)S(1)} %get-tuple-element.25.ws, ...), custom_call_target="tpu_custom_call" | custom-call | flops 1000 | bytes 1000 | tf_op jit(solution)/shard_map/pallas_call | solution.py:246
  16.1 0.0 copy-start
  16.1 0.0 copy-start.1
  16.1 1.6 %collective-permute-done.1.b = f32[256,512]{1,0:T(8,128)S(1)} collective-permute-done((f32[256,512]{1,0:T(8,128)S(1)}, f32[256,512]{1,0:T(8,128)S(1)}, u32[]{:S(2)}, u32[]{:S(2)}) %collective-permute-start.1) | collective-permute-done | bytes 524320 | tf_op jit(solution)/shard_map/ppermute | solution.py:254
  17.7 0.1 shard_map.67.a
  17.8 5.7 %collective-permute-done.2.b = f32[256,512]{1,0:T(8,128)S(1)} collective-permute-done((f32[256,512]{1,0:T(8,128)S(1)}, f32[256,512]{1,0:T(8,128)S(1)}, u32[]{:S(2)}, u32[]{:S(2)}) %collective-permute-start.2) | collective-permute-done | bytes 524320 | tf_op jit(solution)/shard_map/ppermute | solution.py:254
  23.5 0.1 shard_map.69.a
  23.6 0.0 collective-permute-done.3.b
  23.6 0.1 shard_map.71
  23.6 4.2 %collective-permute-start.4 = (f32[64,512]{1,0:T(8,128)S(1)}, f32[64,512]{1,0:T(8,128)S(1)}, u32[]{:S(2)}, u32[]{:S(2)}) collective-permute-start(f32[64,512]{1,0:T(8,128)S(1)} %get-tuple-element.32), channel_id=1, source_target_pairs={{0,35},{1,34},{2,33},{3,32},{4,108},{5,109},{6,110},{7,111},{8,43}... | collective-permute-start | bytes 393224 | tf_op jit(solution)/shard_map/ppermute | solution.py:258
  27.8 0.1 collective-permute-start.5
  27.9 0.6 %collective-permute-start.6 = (f32[64,512]{1,0:T(8,128)S(1)}, f32[64,512]{1,0:T(8,128)S(1)}, u32[]{:S(2)}, u32[]{:S(2)}) collective-permute-start(f32[64,512]{1,0:T(8,128)S(1)} %get-tuple-element.34), channel_id=1, source_target_pairs={{0,3},{1,2},{2,1},{3,0},{4,100},{5,101},{6,102},{7,103},{8,11},{9,... | collective-permute-start | bytes 393224 | tf_op jit(solution)/shard_map/ppermute | solution.py:258
  28.5 2.3 %collective-permute-done.4.b = f32[64,512]{1,0:T(8,128)S(1)} collective-permute-done((f32[64,512]{1,0:T(8,128)S(1)}, f32[64,512]{1,0:T(8,128)S(1)}, u32[]{:S(2)}, u32[]{:S(2)}) %collective-permute-start.4) | collective-permute-done | bytes 131104 | tf_op jit(solution)/shard_map/ppermute | solution.py:258
  30.8 2.0 %collective-permute-done.5.c = f32[64,512]{1,0:T(8,128)S(1)} collective-permute-done((f32[64,512]{1,0:T(8,128)S(1)}, f32[64,512]{1,0:T(8,128)S(1)}, u32[]{:S(2)}, u32[]{:S(2)}) %collective-permute-start.5) | collective-permute-done | bytes 131104 | tf_op jit(solution)/shard_map/ppermute | solution.py:258
  32.8 1.3 %collective-permute-done.6.d = f32[64,512]{1,0:T(8,128)S(1)} collective-permute-done((f32[64,512]{1,0:T(8,128)S(1)}, f32[64,512]{1,0:T(8,128)S(1)}, u32[]{:S(2)}, u32[]{:S(2)}) %collective-permute-start.6) | collective-permute-done | bytes 131104 | tf_op jit(solution)/shard_map/ppermute | solution.py:258
  34.2 6.3 %collective-permute-start.7 = (f32[16,512]{1,0:T(8,128)S(1)}, f32[16,512]{1,0:T(8,128)S(1)}, u32[]{:S(2)}, u32[]{:S(2)}) collective-permute-start(f32[16,512]{1,0:T(8,128)S(1)} %get-tuple-element.36), channel_id=1, source_target_pairs={{0,120},{1,121},{2,122},{3,123},{4,29},{5,28},{6,31},{7,30},{8,112... | collective-permute-start | bytes 98312 | tf_op jit(solution)/shard_map/ppermute | solution.py:260
  40.5 0.5 collective-permute-start.8
  40.9 0.2 collective-permute-start.9
  41.1 1.2 %collective-permute-done.7.b = f32[16,512]{1,0:T(8,128)S(1)} collective-permute-done((f32[16,512]{1,0:T(8,128)S(1)}, f32[16,512]{1,0:T(8,128)S(1)}, u32[]{:S(2)}, u32[]{:S(2)}) %collective-permute-start.7) | collective-permute-done | bytes 32800 | tf_op jit(solution)/shard_map/ppermute | solution.py:260
  42.4 3.2 %collective-permute-done.8.c = f32[16,512]{1,0:T(8,128)S(1)} collective-permute-done((f32[16,512]{1,0:T(8,128)S(1)}, f32[16,512]{1,0:T(8,128)S(1)}, u32[]{:S(2)}, u32[]{:S(2)}) %collective-permute-start.8) | collective-permute-done | bytes 32800 | tf_op jit(solution)/shard_map/ppermute | solution.py:260
  45.6 0.5 collective-permute-done.9.d
  46.1 0.0 copy-done
  46.1 0.0 copy-done.1
  46.1 1.0 %shard_map.73 = f32[8,2,512]{2,1,0:T(2,128)} custom-call(f32[16,512]{1,0:T(8,128)S(1)} %get-tuple-element.35.a, f32[16,512]{1,0:T(8,128)S(1)} %collective-permute-done.7.b, f32[16,512]{1,0:T(8,128)S(1)} %collective-permute-done.8.c, f32[16,512]{1,0:T(8,128)S(1)} %collective-permute-done.9.d, bf16[512,1024]{1,0:T(8,128)(2,1)S(1)} %copy-done.1, ...), custom_call_target="tpu_custom_call" | custom-call | flops 67108864 | bytes 2097152 | tf_op jit(solution)/shard_map/pallas_call | solution.py:261
  (1 shorter events, 0.0 us)
Async XLA Ops:
  0.0 6.2 %collective-permute-start = (f32[32,32,512]{2,1,0:T(8,128)}, f32[32,32,512]{2,1,0:T(8,128)S(1)}, u32[]{:S(2)}, u32[]{:S(2)}) collective-permute-start(f32[32,32,512]{2,1,0:T(8,128)} %param.6), channel_id=1, source_target_pairs={{0,4},{1,5},{2,6},{3,7},{4,0},{5,1},{6,2},{7,3},{8,12},{9,13},{10,... | collective-permute-start | bytes 6291464 | tf_op jit(solution)/shard_map/ppermute | solution.py:220
  7.5 10.2 %collective-permute-start.1 = (f32[256,512]{1,0:T(8,128)S(1)}, f32[256,512]{1,0:T(8,128)S(1)}, u32[]{:S(2)}, u32[]{:S(2)}) collective-permute-start(f32[256,512]{1,0:T(8,128)S(1)} %shard_map.66), channel_id=1, source_target_pairs={{0,9},{1,8},{2,11},{3,10},{4,39},{5,38},{6,37},{7,36},{8,1},{9,0},... | collective-permute-start | bytes 1572872 | tf_op jit(solution)/shard_map/ppermute | solution.py:254
  11.4 12.1 %collective-permute-start.2 = (f32[256,512]{1,0:T(8,128)S(1)}, f32[256,512]{1,0:T(8,128)S(1)}, u32[]{:S(2)}, u32[]{:S(2)}) collective-permute-start(f32[256,512]{1,0:T(8,128)S(1)} %shard_map.68), channel_id=1, source_target_pairs={{0,1},{1,0},{2,3},{3,2},{4,7},{5,6},{6,5},{7,4},{8,9},{9,8},{10,11... | collective-permute-start | bytes 1572872 | tf_op jit(solution)/shard_map/ppermute | solution.py:254
  13.3 10.3 %collective-permute-start.3 = (f32[256,512]{1,0:T(8,128)S(1)}, f32[256,512]{1,0:T(8,128)S(1)}, u32[]{:S(2)}, u32[]{:S(2)}) collective-permute-start(f32[256,512]{1,0:T(8,128)S(1)} %shard_map.70), channel_id=1, source_target_pairs={{0,8},{1,9},{2,10},{3,11},{4,36},{5,37},{6,38},{7,39},{8,0},{9,1},... | collective-permute-start | bytes 1572872 | tf_op jit(solution)/shard_map/ppermute | solution.py:256
  16.1 30.0 %copy-start = (bf16[512,1024]{1,0:T(8,128)(2,1)S(1)}, bf16[512,1024]{1,0:T(8,128)(2,1)}, u32[]{:S(2)}) copy-start(bf16[512,1024]{1,0:T(8,128)(2,1)} %constant.14.clone.t_low) | copy-start | bytes 3145732
  16.1 30.0 %copy-start.1 = (bf16[512,1024]{1,0:T(8,128)(2,1)S(1)}, bf16[512,1024]{1,0:T(8,128)(2,1)}, u32[]{:S(2)}) copy-start(bf16[512,1024]{1,0:T(8,128)(2,1)} %constant.13.clone.t_high) | copy-start | bytes 3145732
  23.6 7.2 %collective-permute-start.4 = (f32[64,512]{1,0:T(8,128)S(1)}, f32[64,512]{1,0:T(8,128)S(1)}, u32[]{:S(2)}, u32[]{:S(2)}) collective-permute-start(f32[64,512]{1,0:T(8,128)S(1)} %get-tuple-element.32), channel_id=1, source_target_pairs={{0,35},{1,34},{2,33},{3,32},{4,108},{5,109},{6,110},{7,111},{8,43}... | collective-permute-start | bytes 393224 | tf_op jit(solution)/shard_map/ppermute | solution.py:258
  27.8 5.0 %collective-permute-start.5 = (f32[64,512]{1,0:T(8,128)S(1)}, f32[64,512]{1,0:T(8,128)S(1)}, u32[]{:S(2)}, u32[]{:S(2)}) collective-permute-start(f32[64,512]{1,0:T(8,128)S(1)} %get-tuple-element.33), channel_id=1, source_target_pairs={{0,32},{1,33},{2,34},{3,35},{4,12},{5,13},{6,14},{7,15},{8,40},{9,... | collective-permute-start | bytes 393224 | tf_op jit(solution)/shard_map/ppermute | solution.py:258
  27.9 6.2 %collective-permute-start.6 = (f32[64,512]{1,0:T(8,128)S(1)}, f32[64,512]{1,0:T(8,128)S(1)}, u32[]{:S(2)}, u32[]{:S(2)}) collective-permute-start(f32[64,512]{1,0:T(8,128)S(1)} %get-tuple-element.34), channel_id=1, source_target_pairs={{0,3},{1,2},{2,1},{3,0},{4,100},{5,101},{6,102},{7,103},{8,11},{9,... | collective-permute-start | bytes 393224 | tf_op jit(solution)/shard_map/ppermute | solution.py:258
  34.2 8.2 %collective-permute-start.7 = (f32[16,512]{1,0:T(8,128)S(1)}, f32[16,512]{1,0:T(8,128)S(1)}, u32[]{:S(2)}, u32[]{:S(2)}) collective-permute-start(f32[16,512]{1,0:T(8,128)S(1)} %get-tuple-element.36), channel_id=1, source_target_pairs={{0,120},{1,121},{2,122},{3,123},{4,29},{5,28},{6,31},{7,30},{8,112... | collective-permute-start | bytes 98312 | tf_op jit(solution)/shard_map/ppermute | solution.py:260
  40.5 5.1 %collective-permute-start.8 = (f32[16,512]{1,0:T(8,128)S(1)}, f32[16,512]{1,0:T(8,128)S(1)}, u32[]{:S(2)}, u32[]{:S(2)}) collective-permute-start(f32[16,512]{1,0:T(8,128)S(1)} %get-tuple-element.37), channel_id=1, source_target_pairs={{0,24},{1,25},{2,26},{3,27},{4,5},{5,4},{6,7},{7,6},{8,16},{9,17},... | collective-permute-start | bytes 98312 | tf_op jit(solution)/shard_map/ppermute | solution.py:260
  40.9 5.1 %collective-permute-start.9 = (f32[16,512]{1,0:T(8,128)S(1)}, f32[16,512]{1,0:T(8,128)S(1)}, u32[]{:S(2)}, u32[]{:S(2)}) collective-permute-start(f32[16,512]{1,0:T(8,128)S(1)} %get-tuple-element.38), channel_id=1, source_target_pairs={{0,96},{1,97},{2,98},{3,99},{4,28},{5,29},{6,30},{7,31},{8,104},{9... | collective-permute-start | bytes 98312 | tf_op jit(solution)/shard_map/ppermute | solution.py:260

commit v2 on v1

--- a/solution.py
+++ b/solution.py
@@ -10,8 +10,10 @@
 from jax.sharding import PartitionSpec as P
 
 AXES = ("scan", "freq")
-X0, X1, Y0, Y1, Z0, Z1 = 1, 2, 4, 8, 16, 32
-STAGES = (((X0, Y0), (Z0, X1), (Y1, Z1)), ((X1, Z0), (Y0, Z1), (X0, Y1)))
+STAGES = (
+    ((16, 32, 48), (1, 4, 5), (2, 8, 10)),
+    ((1, 2, 3), (16, 32, 48), (4, 8, 12)),
+)
 
 
 def gray(place):
@@ -29,16 +31,11 @@
     return ((z * 4 + y) * 2 + core) * 4 + x
 
 
-def flip(core, stage, step):
-    low, high = STAGES[core][stage]
-    return (step & 1) * low | (step >> 1) * high
-
-
 def partners(stage, step):
     pairs = []
     for device in range(128):
         label, core = label_of(device)
-        pairs.append((device, device_of(label ^ flip(core, stage, step), core)))
+        pairs.append((device, device_of(label ^ STAGES[core][stage][step], core)))
     return pairs
 
 
@@ -92,28 +89,27 @@
     where, frames_in, masks_in, aperture_in, phases_in, part, wc, ws, ct, st, ct2, st2, f_high, f_low,
     frames, masks, aperture, phases, a_high, a_low, sems,
 ):
-    copies = [
-        pltpu.make_async_copy(src, dst, sems.at[at])
-        for at, (src, dst) in enumerate(
-            ((frames_in, frames), (masks_in, masks), (aperture_in, aperture), (phases_in, phases))
-        )
-    ]
-    for copy in copies[1:] + copies[:1]:
+    pieces = [pl.ds(at * 128, 128) for at in range(8)]
+    pairs = [(masks_in, masks), (aperture_in, aperture), (phases_in, phases)]
+    pairs += [(frames_in.at[piece, :], frames.at[piece, :]) for piece in pieces]
+    copies = [pltpu.make_async_copy(src, dst, sems.at[at]) for at, (src, dst) in enumerate(pairs)]
+    for copy in copies:
         copy.start()
     scan, freq = where[0], where[1]
     core, y, z = scan & 1, scan >> 1 & 3, scan >> 3
     label = (gray(z) << 4) | (gray(y) << 2) | gray(freq)
     index = iota((64, 128), 0)
-    flips = 0
+    flips = jnp.zeros_like(index)
     for stage in range(3):
-        for low in range(2):
-            bit = jnp.where(core == 0, STAGES[0][stage][low], STAGES[1][stage][low])
-            flips = flips + (index >> (4 - 2 * stage + low) & 1) * bit
+        digit = index >> (4 - 2 * stage) & 3
+        for step in range(3):
+            flip = jnp.where(core == 0, STAGES[0][stage][step], STAGES[1][stage][step])
+            flips = flips ^ jnp.where(digit == step + 1, flip, 0)
     tile = place_of(core, label ^ flips)
     lane_pixel = freq * 32 + (iota((128, 1024), 1) >> 5)
     spread = one_hot(iota((128, 1024), 0) == lane_pixel)
     chosen = one_hot(tile == iota((64, 128), 1))
-    for copy in copies[1:]:
+    for copy in copies[:3]:
         copy.wait()
     mask = dot(chosen, masks[...].astype(jnp.float32).astype(jnp.bfloat16)).astype(jnp.bfloat16)
     mask = dot(mask, spread)
@@ -139,14 +135,14 @@
         c1, s1 = c1[:, None, :], s1[:, None, :]
         c_out[...] = (c1 * c2[None] - s1 * s2[None]).reshape(512, 128)
         s_out[...] = (s1 * c2[None] + c1 * s2[None]).reshape(512, 128)
-    copies[0].wait()
-    f_high[...], f_low[...] = halves(frames[...])
-
-    @pl.loop(1, 4)
-    def _(step):
-        tiles, rows = pl.ds(pl.multiple_of(step * 16, 16), 16), pl.ds(pl.multiple_of(step * 128, 128), 128)
-        fill_matrix(wc[tiles, :], ws[tiles, :], ct[rows, :], st[rows, :], a_high, a_low)
-        part[pl.ds(pl.multiple_of(step * 256, 256), 256), :] = product(a_high, a_low, f_high, f_low)
+    for piece, copy in zip(pieces, copies[3:]):
+        copy.wait()
+        f_high[piece, :], f_low[piece, :] = halves(frames[piece, :])
+    for step in (1, 2, 3):
+        tiles, rows = slice(step * 16, step * 16 + 16), slice(step * 128, step * 128 + 128)
+        high, low = a_high.at[step - 1], a_low.at[step - 1]
+        fill_matrix(wc[tiles, :], ws[tiles, :], ct[rows, :], st[rows, :], high, low)
+        part[step * 256 : step * 256 + 256, :] = product(high, low, f_high, f_low)
 
 
 def later_kernel(step, frames, part, wc, ws, ct, st, out, a_high, a_low, f_high, f_low):
@@ -230,8 +226,8 @@
             pltpu.VMEM((1, 128), jnp.int32),
             pltpu.VMEM((1, 256), jnp.float32),
         ]
-        + [pltpu.VMEM((256, 1024), jnp.bfloat16)] * 2
-        + [pltpu.SemaphoreType.DMA((4,))],
+        + [pltpu.VMEM((3, 256, 1024), jnp.bfloat16)] * 2
+        + [pltpu.SemaphoreType.DMA((11,))],
         cost_estimate=pl.CostEstimate(flops=6 * 768 * 1024 * 512, bytes_accessed=5 << 20, transcendentals=0),
         compiler_params=pltpu.CompilerParams(vmem_limit_bytes=24 << 20),
     )(where, *[pltpu.with_memory_space_constraint(u, pltpu.HBM) for u in (frames.reshape(1024, col_len), intersection_masks, aperture[None, :], phases[None, :])])
@@ -251,13 +247,13 @@
     t_high = table.astype(jnp.bfloat16)
     t_low = (table - t_high.astype(np.float64)).astype(jnp.bfloat16)
     for step in (3, 1):
-        got = lax.ppermute(send[step], AXES, partners(0, step))
+        got = lax.ppermute(send[step], AXES, partners(0, step - 1))
         send[0] = call(add_kernel, block, inputs=2, moved=3 << 19, limit=8 << 20)(send[0], got)
-    got = lax.ppermute(send[2], AXES, partners(0, 2))
+    got = lax.ppermute(send[2], AXES, partners(0, 1))
     send = call(split_kernel, [f32(64, col_len)] * 4, inputs=2, moved=3 << 19, limit=8 << 20)(send[0], got)
-    got = [lax.ppermute(send[step], AXES, partners(1, step)) for step in (3, 1, 2)]
+    got = [lax.ppermute(send[step], AXES, partners(1, step - 1)) for step in (3, 1, 2)]
     send = call(sum_kernel, [f32(16, col_len)] * 4, inputs=4, moved=5 << 17, limit=8 << 20)(send[0], *got)
-    got = [lax.ppermute(send[step], AXES, partners(2, step)) for step in (3, 1, 2)]
+    got = [lax.ppermute(send[step], AXES, partners(2, step - 1)) for step in (3, 1, 2)]
     return call(last_kernel, f32(8, 2, col_len), inputs=6, flops=1 << 26, moved=2 << 20, limit=8 << 20)(
         send[0], *got, jnp.asarray(t_high), jnp.asarray(t_low)
     )

time: 47.2 us -> 44.8 us (0.949)
  waiting for transfers between devices: 17.9 us -> 16.6 us
  starting transfers between devices: 15.6 us -> 14.8 us
    ppermute x9, waiting for transfers between devices: 17.9 us -> 16.6 us  [the longest x2 7.72 us: body(): got = lax.ppermute(send[step], AXES, partners(0, step - 1))]
    ppermute x9, starting transfers between devices: 15.6 us -> 14.8 us  [the longest x3 5.99 us: body(): lax.ppermute(send[step], AXES, partners(2, step - 1))]
  transfers between devices with their start and end apart: 10 -> 10, of which waited for: 8 -> 9; matrix products, arithmetic and copies ran while one was open for 0% -> 0% of each run, Pallas kernels for 24% -> 24%
where the time goes in v2:
time: 44.8 us; the launch traced here: 44.7 us
  waiting for transfers between devices  16.6 us (37%)
  starting transfers between devices  14.8 us (33%)
  Pallas kernels  13.1 us (29%)
    ppermute x2, waiting for transfers between devices, body(): got = lax.ppermute(send[step], AXES, partners(0, step - 1))  7.72 us
    ppermute x3, starting transfers between devices, body(): lax.ppermute(send[step], AXES, partners(2, step - 1))  5.99 us
    pallas_call x1, Pallas kernels, body(): pl.pallas_call(own_kernel, out_shape=[f32(1024, col_len)] + [f32(64, 1024...  5.81 us
    ppermute x2, starting transfers between devices, body(): got = lax.ppermute(send[step], AXES, partners(0, step - 1))  5.14 us
    ppermute x3, waiting for transfers between devices, body(): lax.ppermute(send[step], AXES, partners(1, step - 1))  4.52 us
    ppermute x3, waiting for transfers between devices, body(): lax.ppermute(send[step], AXES, partners(2, step - 1))  4.17 us
    pallas_call x3, Pallas kernels, body(): call(functools.partial(later_kernel, step), block, scratch, inputs=6, **c...  3.73 us
    ppermute x3, starting transfers between devices, body(): lax.ppermute(send[step], AXES, partners(1, step - 1))  3.57 us
  transfers between devices with their start and end apart: 10, of which 9 were waited for; matrix products, arithmetic and copies ran while one was open for 0% of the time, Pallas kernels for 24%

profile of v2, /device:TPU:0, one launch (start us, length us, event | category | flops | bytes accessed | tf_op | source)
XLA Modules:
  0.0 44.7 jit_solution(13494101894749455077)
XLA Ops:
  0.0 0.0 collective-permute-start
  0.0 0.1 pad_add_fusion.where
  0.1 5.8 %shard_map.64 = (f32[1024,512]{1,0:T(8,128)S(1)}, f32[64,1024]{1,0:T(8,128)S(1)}, f32[64,1024]{1,0:T(8,128)S(1)}, f32[512,128]{1,0:T(8,128)S(1)}, f32[512,128]{1...) custom-call(s32[2]{0:T(128)S(1)} %pad_add_fusion.where, ...), custom_call_target="tpu_custom_call" | custom-call | flops 2415919104 | bytes 5242880 | tf_op jit(solution)/shard_map/pallas_call | solution.py:218
  5.9 0.0 collective-permute-done
  5.9 1.2 %shard_map.66 = f32[256,512]{1,0:T(8,128)S(1)} custom-call(f32[1024,512]{1,0:T(8,128)S(1)} %bitcast.6, f32[1024,512]{1,0:T(8,128)S(1)} %get-tuple-element.30.part, f32[64,1024]{1,0:T(8,128)S(1)} %get-tuple-element.24.wc, f32[64,1024]{1,0:T(8,128)S(1)} %get-tuple-element.25.ws, f32[512,128]{1,0:T(8,128)S(1)} %get-tuple-element.28.ct2.ct, ...), custom_call_target="tpu_custom_call" | custom-call | flops 1000 | bytes 1000 | tf_op jit(solution)/shard_map/pallas_call | solution.py:239
  7.2 4.0 %collective-permute-start.1 = (f32[256,512]{1,0:T(8,128)S(1)}, f32[256,512]{1,0:T(8,128)S(1)}, u32[]{:S(2)}, u32[]{:S(2)}) collective-permute-start(f32[256,512]{1,0:T(8,128)S(1)} %shard_map.66), channel_id=1, source_target_pairs={{0,64},{1,65},{2,66},{3,67},{4,6},{5,7},{6,4},{7,5},{8,72},{9,73},... | collective-permute-start | bytes 1572872 | tf_op jit(solution)/shard_map/ppermute | solution.py:250
  11.2 1.2 %shard_map.68 = f32[256,512]{1,0:T(8,128)S(1)} custom-call(f32[1024,512]{1,0:T(8,128)S(1)} %bitcast.7, f32[1024,512]{1,0:T(8,128)S(1)} %get-tuple-element.30.part, f32[64,1024]{1,0:T(8,128)S(1)} %get-tuple-element.24.wc, f32[64,1024]{1,0:T(8,128)S(1)} %get-tuple-element.25.ws, f32[512,128]{1,0:T(8,128)S(1)} %get-tuple-element.28.ct2.ct, ...), custom_call_target="tpu_custom_call" | custom-call | flops 1000 | bytes 1000 | tf_op jit(solution)/shard_map/pallas_call | solution.py:239
  12.4 1.1 %collective-permute-start.2 = (f32[256,512]{1,0:T(8,128)S(1)}, f32[256,512]{1,0:T(8,128)S(1)}, u32[]{:S(2)}, u32[]{:S(2)}) collective-permute-start(f32[256,512]{1,0:T(8,128)S(1)} %shard_map.68), channel_id=1, source_target_pairs={{0,32},{1,33},{2,34},{3,35},{4,5},{5,4},{6,7},{7,6},{8,40},{9,41},... | collective-permute-start | bytes 1572872 | tf_op jit(solution)/shard_map/ppermute | solution.py:250
  13.6 1.2 %shard_map.70 = f32[256,512]{1,0:T(8,128)S(1)} custom-call(f32[1024,512]{1,0:T(8,128)S(1)} %bitcast.8, f32[1024,512]{1,0:T(8,128)S(1)} %get-tuple-element.30.part, f32[64,1024]{1,0:T(8,128)S(1)} %get-tuple-element.24.wc, f32[64,1024]{1,0:T(8,128)S(1)} %get-tuple-element.25.ws, f32[512,128]{1,0:T(8,128)S(1)} %get-tuple-element.28.ct2.ct, ...), custom_call_target="tpu_custom_call" | custom-call | flops 1000 | bytes 1000 | tf_op jit(solution)/shard_map/pallas_call | solution.py:239
  14.8 0.1 collective-permute-start.3
  14.9 2.3 %shard_map.65.a = f32[256,512]{1,0:T(8,128)S(1)} custom-call(bf16[1024,512]{1,0:T(8,128)(2,1)S(1)} %get-tuple-element.22.own_high, bf16[1024,512]{1,0:T(8,128)(2,1)S(1)} %get-tuple-element.23.own_low, f32[1024,512]{1,0:T(8,128)S(1)} %bitcast.9, f32[64,1024]{1,0:T(8,128)S(1)} %get-tuple-element.24.wc, f32[64,1024]{1,0:T(8,128)S(1)} %get-tuple-element.25.ws, ...), custom_call_target="tpu_custom_call" | custom-call | flops 1000 | bytes 1000 | tf_op jit(solution)/shard_map/pallas_call | solution.py:242
  17.2 0.0 copy-start
  17.2 0.0 copy-start.1
  17.3 1.1 %collective-permute-done.1.b = f32[256,512]{1,0:T(8,128)S(1)} collective-permute-done((f32[256,512]{1,0:T(8,128)S(1)}, f32[256,512]{1,0:T(8,128)S(1)}, u32[]{:S(2)}, u32[]{:S(2)}) %collective-permute-start.1) | collective-permute-done | bytes 524320 | tf_op jit(solution)/shard_map/ppermute | solution.py:250
  18.4 0.1 shard_map.67.a
  18.4 6.6 %collective-permute-done.2.b = f32[256,512]{1,0:T(8,128)S(1)} collective-permute-done((f32[256,512]{1,0:T(8,128)S(1)}, f32[256,512]{1,0:T(8,128)S(1)}, u32[]{:S(2)}, u32[]{:S(2)}) %collective-permute-start.2) | collective-permute-done | bytes 524320 | tf_op jit(solution)/shard_map/ppermute | solution.py:250
  25.0 0.1 shard_map.69.a
  25.1 0.2 collective-permute-done.3.b
  25.3 0.1 shard_map.71
  25.3 2.6 %collective-permute-start.4 = (f32[64,512]{1,0:T(8,128)S(1)}, f32[64,512]{1,0:T(8,128)S(1)}, u32[]{:S(2)}, u32[]{:S(2)}) collective-permute-start(f32[64,512]{1,0:T(8,128)S(1)} %get-tuple-element.32), channel_id=1, source_target_pairs={{0,9},{1,8},{2,11},{3,10},{4,68},{5,69},{6,70},{7,71},{8,1},{9,0},... | collective-permute-start | bytes 393224 | tf_op jit(solution)/shard_map/ppermute | solution.py:254
  27.9 0.5 %collective-permute-start.5 = (f32[64,512]{1,0:T(8,128)S(1)}, f32[64,512]{1,0:T(8,128)S(1)}, u32[]{:S(2)}, u32[]{:S(2)}) collective-permute-start(f32[64,512]{1,0:T(8,128)S(1)} %get-tuple-element.33), channel_id=1, source_target_pairs={{0,1},{1,0},{2,3},{3,2},{4,36},{5,37},{6,38},{7,39},{8,9},{9,8},{1... | collective-permute-start | bytes 393224 | tf_op jit(solution)/shard_map/ppermute | solution.py:254
  28.5 0.5 %collective-permute-start.6 = (f32[64,512]{1,0:T(8,128)S(1)}, f32[64,512]{1,0:T(8,128)S(1)}, u32[]{:S(2)}, u32[]{:S(2)}) collective-permute-start(f32[64,512]{1,0:T(8,128)S(1)} %get-tuple-element.34), channel_id=1, source_target_pairs={{0,8},{1,9},{2,10},{3,11},{4,100},{5,101},{6,102},{7,103},{8,0},{9... | collective-permute-start | bytes 393224 | tf_op jit(solution)/shard_map/ppermute | solution.py:254
  28.9 2.4 %collective-permute-done.4.b = f32[64,512]{1,0:T(8,128)S(1)} collective-permute-done((f32[64,512]{1,0:T(8,128)S(1)}, f32[64,512]{1,0:T(8,128)S(1)}, u32[]{:S(2)}, u32[]{:S(2)}) %collective-permute-start.4) | collective-permute-done | bytes 131104 | tf_op jit(solution)/shard_map/ppermute | solution.py:254
  31.3 1.6 %collective-permute-done.5.c = f32[64,512]{1,0:T(8,128)S(1)} collective-permute-done((f32[64,512]{1,0:T(8,128)S(1)}, f32[64,512]{1,0:T(8,128)S(1)}, u32[]{:S(2)}, u32[]{:S(2)}) %collective-permute-start.5) | collective-permute-done | bytes 131104 | tf_op jit(solution)/shard_map/ppermute | solution.py:254
  32.9 0.5 %collective-permute-done.6.d = f32[64,512]{1,0:T(8,128)S(1)} collective-permute-done((f32[64,512]{1,0:T(8,128)S(1)}, f32[64,512]{1,0:T(8,128)S(1)}, u32[]{:S(2)}, u32[]{:S(2)}) %collective-permute-start.6) | collective-permute-done | bytes 131104 | tf_op jit(solution)/shard_map/ppermute | solution.py:254
  33.5 4.5 %collective-permute-start.7 = (f32[16,512]{1,0:T(8,128)S(1)}, f32[16,512]{1,0:T(8,128)S(1)}, u32[]{:S(2)}, u32[]{:S(2)}) collective-permute-start(f32[16,512]{1,0:T(8,128)S(1)} %get-tuple-element.36), channel_id=1, source_target_pairs={{0,27},{1,26},{2,25},{3,24},{4,20},{5,21},{6,22},{7,23},{8,19},{9,... | collective-permute-start | bytes 98312 | tf_op jit(solution)/shard_map/ppermute | solution.py:256
  38.0 0.5 %collective-permute-start.8 = (f32[16,512]{1,0:T(8,128)S(1)}, f32[16,512]{1,0:T(8,128)S(1)}, u32[]{:S(2)}, u32[]{:S(2)}) collective-permute-start(f32[16,512]{1,0:T(8,128)S(1)} %get-tuple-element.37), channel_id=1, source_target_pairs={{0,3},{1,2},{2,1},{3,0},{4,12},{5,13},{6,14},{7,15},{8,11},{9,10},... | collective-permute-start | bytes 98312 | tf_op jit(solution)/shard_map/ppermute | solution.py:256
  38.5 1.0 %collective-permute-start.9 = (f32[16,512]{1,0:T(8,128)S(1)}, f32[16,512]{1,0:T(8,128)S(1)}, u32[]{:S(2)}, u32[]{:S(2)}) collective-permute-start(f32[16,512]{1,0:T(8,128)S(1)} %get-tuple-element.38), channel_id=1, source_target_pairs={{0,24},{1,25},{2,26},{3,27},{4,28},{5,29},{6,30},{7,31},{8,16},{9,... | collective-permute-start | bytes 98312 | tf_op jit(solution)/shard_map/ppermute | solution.py:256
  39.4 1.4 %collective-permute-done.7.b = f32[16,512]{1,0:T(8,128)S(1)} collective-permute-done((f32[16,512]{1,0:T(8,128)S(1)}, f32[16,512]{1,0:T(8,128)S(1)}, u32[]{:S(2)}, u32[]{:S(2)}) %collective-permute-start.7) | collective-permute-done | bytes 32800 | tf_op jit(solution)/shard_map/ppermute | solution.py:256
  40.9 2.2 %collective-permute-done.8.c = f32[16,512]{1,0:T(8,128)S(1)} collective-permute-done((f32[16,512]{1,0:T(8,128)S(1)}, f32[16,512]{1,0:T(8,128)S(1)}, u32[]{:S(2)}, u32[]{:S(2)}) %collective-permute-start.8) | collective-permute-done | bytes 32800 | tf_op jit(solution)/shard_map/ppermute | solution.py:256
  43.1 0.5 %collective-permute-done.9.d = f32[16,512]{1,0:T(8,128)S(1)} collective-permute-done((f32[16,512]{1,0:T(8,128)S(1)}, f32[16,512]{1,0:T(8,128)S(1)}, u32[]{:S(2)}, u32[]{:S(2)}) %collective-permute-start.9) | collective-permute-done | bytes 32800 | tf_op jit(solution)/shard_map/ppermute | solution.py:256
  43.6 0.0 copy-done
  43.6 0.0 copy-done.1
  43.6 1.0 %shard_map.73 = f32[8,2,512]{2,1,0:T(2,128)} custom-call(f32[16,512]{1,0:T(8,128)S(1)} %get-tuple-element.35.a, f32[16,512]{1,0:T(8,128)S(1)} %collective-permute-done.7.b, f32[16,512]{1,0:T(8,128)S(1)} %collective-permute-done.8.c, f32[16,512]{1,0:T(8,128)S(1)} %collective-permute-done.9.d, bf16[512,1024]{1,0:T(8,128)(2,1)S(1)} %copy-done.1, ...), custom_call_target="tpu_custom_call" | custom-call | flops 67108864 | bytes 2097152 | tf_op jit(solution)/shard_map/pallas_call | solution.py:257
  (1 shorter events, 0.0 us)
Async XLA Ops:
  0.0 5.9 %collective-permute-start = (f32[32,32,512]{2,1,0:T(8,128)}, f32[32,32,512]{2,1,0:T(8,128)S(1)}, u32[]{:S(2)}, u32[]{:S(2)}) collective-permute-start(f32[32,32,512]{2,1,0:T(8,128)} %param.6), channel_id=1, source_target_pairs={{0,4},{1,5},{2,6},{3,7},{4,0},{5,1},{6,2},{7,3},{8,12},{9,13},{10,... | collective-permute-start | bytes 6291464 | tf_op jit(solution)/shard_map/ppermute | solution.py:216
  7.2 11.2 %collective-permute-start.1 = (f32[256,512]{1,0:T(8,128)S(1)}, f32[256,512]{1,0:T(8,128)S(1)}, u32[]{:S(2)}, u32[]{:S(2)}) collective-permute-start(f32[256,512]{1,0:T(8,128)S(1)} %shard_map.66), channel_id=1, source_target_pairs={{0,64},{1,65},{2,66},{3,67},{4,6},{5,7},{6,4},{7,5},{8,72},{9,73},... | collective-permute-start | bytes 1572872 | tf_op jit(solution)/shard_map/ppermute | solution.py:250
  12.4 12.6 %collective-permute-start.2 = (f32[256,512]{1,0:T(8,128)S(1)}, f32[256,512]{1,0:T(8,128)S(1)}, u32[]{:S(2)}, u32[]{:S(2)}) collective-permute-start(f32[256,512]{1,0:T(8,128)S(1)} %shard_map.68), channel_id=1, source_target_pairs={{0,32},{1,33},{2,34},{3,35},{4,5},{5,4},{6,7},{7,6},{8,40},{9,41},... | collective-permute-start | bytes 1572872 | tf_op jit(solution)/shard_map/ppermute | solution.py:250
  14.8 10.5 %collective-permute-start.3 = (f32[256,512]{1,0:T(8,128)S(1)}, f32[256,512]{1,0:T(8,128)S(1)}, u32[]{:S(2)}, u32[]{:S(2)}) collective-permute-start(f32[256,512]{1,0:T(8,128)S(1)} %shard_map.70), channel_id=1, source_target_pairs={{0,96},{1,97},{2,98},{3,99},{4,7},{5,6},{6,5},{7,4},{8,104},{9,105... | collective-permute-start | bytes 1572872 | tf_op jit(solution)/shard_map/ppermute | solution.py:252
  17.2 26.4 %copy-start = (bf16[512,1024]{1,0:T(8,128)(2,1)S(1)}, bf16[512,1024]{1,0:T(8,128)(2,1)}, u32[]{:S(2)}) copy-start(bf16[512,1024]{1,0:T(8,128)(2,1)} %constant.14.clone.t_low) | copy-start | bytes 3145732
  17.2 26.4 %copy-start.1 = (bf16[512,1024]{1,0:T(8,128)(2,1)S(1)}, bf16[512,1024]{1,0:T(8,128)(2,1)}, u32[]{:S(2)}) copy-start(bf16[512,1024]{1,0:T(8,128)(2,1)} %constant.13.clone.t_high) | copy-start | bytes 3145732
  25.3 5.9 %collective-permute-start.4 = (f32[64,512]{1,0:T(8,128)S(1)}, f32[64,512]{1,0:T(8,128)S(1)}, u32[]{:S(2)}, u32[]{:S(2)}) collective-permute-start(f32[64,512]{1,0:T(8,128)S(1)} %get-tuple-element.32), channel_id=1, source_target_pairs={{0,9},{1,8},{2,11},{3,10},{4,68},{5,69},{6,70},{7,71},{8,1},{9,0},... | collective-permute-start | bytes 393224 | tf_op jit(solution)/shard_map/ppermute | solution.py:254
  27.9 5.0 %collective-permute-start.5 = (f32[64,512]{1,0:T(8,128)S(1)}, f32[64,512]{1,0:T(8,128)S(1)}, u32[]{:S(2)}, u32[]{:S(2)}) collective-permute-start(f32[64,512]{1,0:T(8,128)S(1)} %get-tuple-element.33), channel_id=1, source_target_pairs={{0,1},{1,0},{2,3},{3,2},{4,36},{5,37},{6,38},{7,39},{8,9},{9,8},{1... | collective-permute-start | bytes 393224 | tf_op jit(solution)/shard_map/ppermute | solution.py:254
  28.5 5.0 %collective-permute-start.6 = (f32[64,512]{1,0:T(8,128)S(1)}, f32[64,512]{1,0:T(8,128)S(1)}, u32[]{:S(2)}, u32[]{:S(2)}) collective-permute-start(f32[64,512]{1,0:T(8,128)S(1)} %get-tuple-element.34), channel_id=1, source_target_pairs={{0,8},{1,9},{2,10},{3,11},{4,100},{5,101},{6,102},{7,103},{8,0},{9... | collective-permute-start | bytes 393224 | tf_op jit(solution)/shard_map/ppermute | solution.py:254
  33.5 7.4 %collective-permute-start.7 = (f32[16,512]{1,0:T(8,128)S(1)}, f32[16,512]{1,0:T(8,128)S(1)}, u32[]{:S(2)}, u32[]{:S(2)}) collective-permute-start(f32[16,512]{1,0:T(8,128)S(1)} %get-tuple-element.36), channel_id=1, source_target_pairs={{0,27},{1,26},{2,25},{3,24},{4,20},{5,21},{6,22},{7,23},{8,19},{9,... | collective-permute-start | bytes 98312 | tf_op jit(solution)/shard_map/ppermute | solution.py:256
  38.0 5.1 %collective-permute-start.8 = (f32[16,512]{1,0:T(8,128)S(1)}, f32[16,512]{1,0:T(8,128)S(1)}, u32[]{:S(2)}, u32[]{:S(2)}) collective-permute-start(f32[16,512]{1,0:T(8,128)S(1)} %get-tuple-element.37), channel_id=1, source_target_pairs={{0,3},{1,2},{2,1},{3,0},{4,12},{5,13},{6,14},{7,15},{8,11},{9,10},... | collective-permute-start | bytes 98312 | tf_op jit(solution)/shard_map/ppermute | solution.py:256
  38.5 5.1 %collective-permute-start.9 = (f32[16,512]{1,0:T(8,128)S(1)}, f32[16,512]{1,0:T(8,128)S(1)}, u32[]{:S(2)}, u32[]{:S(2)}) collective-permute-start(f32[16,512]{1,0:T(8,128)S(1)} %get-tuple-element.38), channel_id=1, source_target_pairs={{0,24},{1,25},{2,26},{3,27},{4,28},{5,29},{6,30},{7,31},{8,16},{9,... | collective-permute-start | bytes 98312 | tf_op jit(solution)/shard_map/ppermute | solution.py:256

commit v3 on v2

--- a/solution.py
+++ b/solution.py
@@ -11,7 +11,7 @@
 
 AXES = ("scan", "freq")
 STAGES = (
-    ((16, 32, 48), (1, 4, 5), (2, 8, 10)),
+    ((16, 32, 48), (2, 8, 10), (1, 4, 5)),
     ((1, 2, 3), (16, 32, 48), (4, 8, 12)),
 )
 
@@ -237,7 +237,7 @@
     block = f32(256, col_len)
     send = {
         step: call(functools.partial(later_kernel, step), block, scratch, inputs=6, **cost)(other, part, wc, ws, ct2, st2)
-        for step in (3, 1, 2)
+        for step in (3, 2, 1)
     }
     send[0] = call(near_kernel, block, scratch, inputs=9, **cost)(f_high, f_low, other, wc, ws, ct, st, ct2, st2)
     columns = np.arange(col_len)
@@ -246,14 +246,14 @@
     table = np.concatenate([np.cos(angle), np.sin(angle)], 1) * scale
     t_high = table.astype(jnp.bfloat16)
     t_low = (table - t_high.astype(np.float64)).astype(jnp.bfloat16)
-    for step in (3, 1):
+    for step in (3, 2):
         got = lax.ppermute(send[step], AXES, partners(0, step - 1))
         send[0] = call(add_kernel, block, inputs=2, moved=3 << 19, limit=8 << 20)(send[0], got)
-    got = lax.ppermute(send[2], AXES, partners(0, 1))
+    got = lax.ppermute(send[1], AXES, partners(0, 0))
     send = call(split_kernel, [f32(64, col_len)] * 4, inputs=2, moved=3 << 19, limit=8 << 20)(send[0], got)
-    got = [lax.ppermute(send[step], AXES, partners(1, step - 1)) for step in (3, 1, 2)]
+    got = [lax.ppermute(send[step], AXES, partners(1, step - 1)) for step in (3, 2, 1)]
     send = call(sum_kernel, [f32(16, col_len)] * 4, inputs=4, moved=5 << 17, limit=8 << 20)(send[0], *got)
-    got = [lax.ppermute(send[step], AXES, partners(2, step - 1)) for step in (3, 1, 2)]
+    got = [lax.ppermute(send[step], AXES, partners(2, step - 1)) for step in (3, 2, 1)]
     return call(last_kernel, f32(8, 2, col_len), inputs=6, flops=1 << 26, moved=2 << 20, limit=8 << 20)(
         send[0], *got, jnp.asarray(t_high), jnp.asarray(t_low)
     )

time: 44.8 us -> 43.9 us (0.980)
  waiting for transfers between devices: 16.6 us -> 15.3 us
    ppermute x3, starting transfers between devices: 5.99 us -> 3.56 us  [body(): lax.ppermute(send[step], AXES, partners(2, step - 1))]
    ppermute x3, starting transfers between devices: 3.57 us -> 5.99 us  [body(): lax.ppermute(send[step], AXES, partners(1, step - 1))]
    ppermute x3, waiting for transfers between devices: 4.17 us -> 1.89 us  [body(): lax.ppermute(send[step], AXES, partners(2, step - 1))]
    ppermute x3, waiting for transfers between devices: 4.52 us -> 5.71 us  [body(): lax.ppermute(send[step], AXES, partners(1, step - 1))]
    ppermute x2, waiting for transfers between devices: 7.72 us -> 6.66 us  [body(): got = lax.ppermute(send[step], AXES, partners(0, step - 1))]
    ppermute x1, waiting for transfers between devices: 0.18 us -> 1 us  [body(): got = lax.ppermute(send[1], AXES, partners(0, 0))]
  transfers between devices with their start and end apart: 10 -> 10, of which waited for: 9 -> 8; matrix products, arithmetic and copies ran while one was open for 0% -> 0% of each run, Pallas kernels for 24% -> 25%
where the time goes in v3:
time: 43.9 us; the launch traced here: 43.3 us
  waiting for transfers between devices  15.3 us (35%)
  starting transfers between devices  14.8 us (34%)
  Pallas kernels  13.1 us (30%)
    ppermute x2, waiting for transfers between devices, body(): got = lax.ppermute(send[step], AXES, partners(0, step - 1))  6.66 us
    ppermute x3, starting transfers between devices, body(): lax.ppermute(send[step], AXES, partners(1, step - 1))  5.99 us
    pallas_call x1, Pallas kernels, body(): pl.pallas_call(own_kernel, out_shape=[f32(1024, col_len)] + [f32(64, 1024...  5.81 us
    ppermute x3, waiting for transfers between devices, body(): lax.ppermute(send[step], AXES, partners(1, step - 1))  5.71 us
    ppermute x2, starting transfers between devices, body(): got = lax.ppermute(send[step], AXES, partners(0, step - 1))  4.82 us
    pallas_call x3, Pallas kernels, body(): call(functools.partial(later_kernel, step), block, scratch, inputs=6, **c...  3.74 us
    ppermute x3, starting transfers between devices, body(): lax.ppermute(send[step], AXES, partners(2, step - 1))  3.56 us
    pallas_call x1, Pallas kernels, body(): call(near_kernel, block, scratch, inputs=9, **cost)  2.33 us
  transfers between devices with their start and end apart: 10, of which 8 were waited for; matrix products, arithmetic and copies ran while one was open for 0% of the time, Pallas kernels for 25%

profile of v3, /device:TPU:0, one launch (start us, length us, event | category | flops | bytes accessed | tf_op | source)
XLA Modules:
  0.0 43.3 jit_solution(7456016763077435168)
XLA Ops:
  0.0 0.0 collective-permute-start
  0.0 0.1 pad_add_fusion.where
  0.1 5.8 %shard_map.64 = (f32[1024,512]{1,0:T(8,128)S(1)}, f32[64,1024]{1,0:T(8,128)S(1)}, f32[64,1024]{1,0:T(8,128)S(1)}, f32[512,128]{1,0:T(8,128)S(1)}, f32[512,128]{1...) custom-call(s32[2]{0:T(128)S(1)} %pad_add_fusion.where, ...), custom_call_target="tpu_custom_call" | custom-call | flops 2415919104 | bytes 5242880 | tf_op jit(solution)/shard_map/pallas_call | solution.py:218
  5.9 0.0 collective-permute-done
  5.9 1.2 %shard_map.66 = f32[256,512]{1,0:T(8,128)S(1)} custom-call(f32[1024,512]{1,0:T(8,128)S(1)} %bitcast.6, f32[1024,512]{1,0:T(8,128)S(1)} %get-tuple-element.30.part, f32[64,1024]{1,0:T(8,128)S(1)} %get-tuple-element.24.wc, f32[64,1024]{1,0:T(8,128)S(1)} %get-tuple-element.25.ws, f32[512,128]{1,0:T(8,128)S(1)} %get-tuple-element.28.ct2.ct, ...), custom_call_target="tpu_custom_call" | custom-call | flops 1000 | bytes 1000 | tf_op jit(solution)/shard_map/pallas_call | solution.py:239
  7.2 4.0 %collective-permute-start.1 = (f32[256,512]{1,0:T(8,128)S(1)}, f32[256,512]{1,0:T(8,128)S(1)}, u32[]{:S(2)}, u32[]{:S(2)}) collective-permute-start(f32[256,512]{1,0:T(8,128)S(1)} %shard_map.66), channel_id=1, source_target_pairs={{0,64},{1,65},{2,66},{3,67},{4,6},{5,7},{6,4},{7,5},{8,72},{9,73},... | collective-permute-start | bytes 1572872 | tf_op jit(solution)/shard_map/ppermute | solution.py:250
  11.2 1.2 %shard_map.68 = f32[256,512]{1,0:T(8,128)S(1)} custom-call(f32[1024,512]{1,0:T(8,128)S(1)} %bitcast.7, f32[1024,512]{1,0:T(8,128)S(1)} %get-tuple-element.30.part, f32[64,1024]{1,0:T(8,128)S(1)} %get-tuple-element.24.wc, f32[64,1024]{1,0:T(8,128)S(1)} %get-tuple-element.25.ws, f32[512,128]{1,0:T(8,128)S(1)} %get-tuple-element.28.ct2.ct, ...), custom_call_target="tpu_custom_call" | custom-call | flops 1000 | bytes 1000 | tf_op jit(solution)/shard_map/pallas_call | solution.py:239
  12.4 0.8 %collective-permute-start.2 = (f32[256,512]{1,0:T(8,128)S(1)}, f32[256,512]{1,0:T(8,128)S(1)}, u32[]{:S(2)}, u32[]{:S(2)}) collective-permute-start(f32[256,512]{1,0:T(8,128)S(1)} %shard_map.68), channel_id=1, source_target_pairs={{0,96},{1,97},{2,98},{3,99},{4,7},{5,6},{6,5},{7,4},{8,104},{9,105... | collective-permute-start | bytes 1572872 | tf_op jit(solution)/shard_map/ppermute | solution.py:250
  13.2 1.2 %shard_map.70 = f32[256,512]{1,0:T(8,128)S(1)} custom-call(f32[1024,512]{1,0:T(8,128)S(1)} %bitcast.8, f32[1024,512]{1,0:T(8,128)S(1)} %get-tuple-element.30.part, f32[64,1024]{1,0:T(8,128)S(1)} %get-tuple-element.24.wc, f32[64,1024]{1,0:T(8,128)S(1)} %get-tuple-element.25.ws, f32[512,128]{1,0:T(8,128)S(1)} %get-tuple-element.28.ct2.ct, ...), custom_call_target="tpu_custom_call" | custom-call | flops 1000 | bytes 1000 | tf_op jit(solution)/shard_map/pallas_call | solution.py:239
  14.5 0.4 collective-permute-start.3
  14.9 2.3 %shard_map.65.a = f32[256,512]{1,0:T(8,128)S(1)} custom-call(bf16[1024,512]{1,0:T(8,128)(2,1)S(1)} %get-tuple-element.22.own_high, bf16[1024,512]{1,0:T(8,128)(2,1)S(1)} %get-tuple-element.23.own_low, f32[1024,512]{1,0:T(8,128)S(1)} %bitcast.9, f32[64,1024]{1,0:T(8,128)S(1)} %get-tuple-element.24.wc, f32[64,1024]{1,0:T(8,128)S(1)} %get-tuple-element.25.ws, ...), custom_call_target="tpu_custom_call" | custom-call | flops 1000 | bytes 1000 | tf_op jit(solution)/shard_map/pallas_call | solution.py:242
  17.2 0.0 copy-start
  17.2 0.0 copy-start.1
  17.3 1.2 %collective-permute-done.1.b = f32[256,512]{1,0:T(8,128)S(1)} collective-permute-done((f32[256,512]{1,0:T(8,128)S(1)}, f32[256,512]{1,0:T(8,128)S(1)}, u32[]{:S(2)}, u32[]{:S(2)}) %collective-permute-start.1) | collective-permute-done | bytes 524320 | tf_op jit(solution)/shard_map/ppermute | solution.py:250
  18.5 0.1 shard_map.67.a
  18.5 5.5 %collective-permute-done.2.b = f32[256,512]{1,0:T(8,128)S(1)} collective-permute-done((f32[256,512]{1,0:T(8,128)S(1)}, f32[256,512]{1,0:T(8,128)S(1)}, u32[]{:S(2)}, u32[]{:S(2)}) %collective-permute-start.2) | collective-permute-done | bytes 524320 | tf_op jit(solution)/shard_map/ppermute | solution.py:250
  24.0 0.1 shard_map.69.a
  24.0 1.0 %collective-permute-done.3.b = f32[256,512]{1,0:T(8,128)S(1)} collective-permute-done((f32[256,512]{1,0:T(8,128)S(1)}, f32[256,512]{1,0:T(8,128)S(1)}, u32[]{:S(2)}, u32[]{:S(2)}) %collective-permute-start.3) | collective-permute-done | bytes 524320 | tf_op jit(solution)/shard_map/ppermute | solution.py:252
  25.0 0.1 shard_map.71
  25.1 5.3 %collective-permute-start.4 = (f32[64,512]{1,0:T(8,128)S(1)}, f32[64,512]{1,0:T(8,128)S(1)}, u32[]{:S(2)}, u32[]{:S(2)}) collective-permute-start(f32[64,512]{1,0:T(8,128)S(1)} %get-tuple-element.32), channel_id=1, source_target_pairs={{0,27},{1,26},{2,25},{3,24},{4,68},{5,69},{6,70},{7,71},{8,19},{9,... | collective-permute-start | bytes 393224 | tf_op jit(solution)/shard_map/ppermute | solution.py:254
  30.4 0.2 collective-permute-start.5
  30.6 0.5 %collective-permute-start.6 = (f32[64,512]{1,0:T(8,128)S(1)}, f32[64,512]{1,0:T(8,128)S(1)}, u32[]{:S(2)}, u32[]{:S(2)}) collective-permute-start(f32[64,512]{1,0:T(8,128)S(1)} %get-tuple-element.34), channel_id=1, source_target_pairs={{0,3},{1,2},{2,1},{3,0},{4,36},{5,37},{6,38},{7,39},{8,11},{9,10},... | collective-permute-start | bytes 393224 | tf_op jit(solution)/shard_map/ppermute | solution.py:254
  31.1 2.4 %collective-permute-done.4.b = f32[64,512]{1,0:T(8,128)S(1)} collective-permute-done((f32[64,512]{1,0:T(8,128)S(1)}, f32[64,512]{1,0:T(8,128)S(1)}, u32[]{:S(2)}, u32[]{:S(2)}) %collective-permute-start.4) | collective-permute-done | bytes 131104 | tf_op jit(solution)/shard_map/ppermute | solution.py:254
  33.5 3.1 %collective-permute-done.5.c = f32[64,512]{1,0:T(8,128)S(1)} collective-permute-done((f32[64,512]{1,0:T(8,128)S(1)}, f32[64,512]{1,0:T(8,128)S(1)}, u32[]{:S(2)}, u32[]{:S(2)}) %collective-permute-start.5) | collective-permute-done | bytes 131104 | tf_op jit(solution)/shard_map/ppermute | solution.py:254
  36.6 0.2 collective-permute-done.6.d
  36.8 0.1 collective-permute-start.7
  36.9 1.4 %collective-permute-start.8 = (f32[16,512]{1,0:T(8,128)S(1)}, f32[16,512]{1,0:T(8,128)S(1)}, u32[]{:S(2)}, u32[]{:S(2)}) collective-permute-start(f32[16,512]{1,0:T(8,128)S(1)} %get-tuple-element.37), channel_id=1, source_target_pairs={{0,8},{1,9},{2,10},{3,11},{4,28},{5,29},{6,30},{7,31},{8,0},{9,1},... | collective-permute-start | bytes 98312 | tf_op jit(solution)/shard_map/ppermute | solution.py:256
  38.4 2.0 %collective-permute-start.9 = (f32[16,512]{1,0:T(8,128)S(1)}, f32[16,512]{1,0:T(8,128)S(1)}, u32[]{:S(2)}, u32[]{:S(2)}) collective-permute-start(f32[16,512]{1,0:T(8,128)S(1)} %get-tuple-element.38), channel_id=1, source_target_pairs={{0,1},{1,0},{2,3},{3,2},{4,12},{5,13},{6,14},{7,15},{8,9},{9,8},{1... | collective-permute-start | bytes 98312 | tf_op jit(solution)/shard_map/ppermute | solution.py:256
  40.4 1.3 %collective-permute-done.7.b = f32[16,512]{1,0:T(8,128)S(1)} collective-permute-done((f32[16,512]{1,0:T(8,128)S(1)}, f32[16,512]{1,0:T(8,128)S(1)}, u32[]{:S(2)}, u32[]{:S(2)}) %collective-permute-start.7) | collective-permute-done | bytes 32800 | tf_op jit(solution)/shard_map/ppermute | solution.py:256
  41.7 0.0 collective-permute-done.8.c
  41.7 0.6 %collective-permute-done.9.d = f32[16,512]{1,0:T(8,128)S(1)} collective-permute-done((f32[16,512]{1,0:T(8,128)S(1)}, f32[16,512]{1,0:T(8,128)S(1)}, u32[]{:S(2)}, u32[]{:S(2)}) %collective-permute-start.9) | collective-permute-done | bytes 32800 | tf_op jit(solution)/shard_map/ppermute | solution.py:256
  42.3 0.0 copy-done
  42.3 0.0 copy-done.1
  42.3 1.0 %shard_map.73 = f32[8,2,512]{2,1,0:T(2,128)} custom-call(f32[16,512]{1,0:T(8,128)S(1)} %get-tuple-element.35.a, f32[16,512]{1,0:T(8,128)S(1)} %collective-permute-done.7.b, f32[16,512]{1,0:T(8,128)S(1)} %collective-permute-done.8.c, f32[16,512]{1,0:T(8,128)S(1)} %collective-permute-done.9.d, bf16[512,1024]{1,0:T(8,128)(2,1)S(1)} %copy-done.1, ...), custom_call_target="tpu_custom_call" | custom-call | flops 67108864 | bytes 2097152 | tf_op jit(solution)/shard_map/pallas_call | solution.py:257
  (1 shorter events, 0.0 us)
Async XLA Ops:
  0.0 5.9 %collective-permute-start = (f32[32,32,512]{2,1,0:T(8,128)}, f32[32,32,512]{2,1,0:T(8,128)S(1)}, u32[]{:S(2)}, u32[]{:S(2)}) collective-permute-start(f32[32,32,512]{2,1,0:T(8,128)} %param.6), channel_id=1, source_target_pairs={{0,4},{1,5},{2,6},{3,7},{4,0},{5,1},{6,2},{7,3},{8,12},{9,13},{10,... | collective-permute-start | bytes 6291464 | tf_op jit(solution)/shard_map/ppermute | solution.py:216
  7.2 11.3 %collective-permute-start.1 = (f32[256,512]{1,0:T(8,128)S(1)}, f32[256,512]{1,0:T(8,128)S(1)}, u32[]{:S(2)}, u32[]{:S(2)}) collective-permute-start(f32[256,512]{1,0:T(8,128)S(1)} %shard_map.66), channel_id=1, source_target_pairs={{0,64},{1,65},{2,66},{3,67},{4,6},{5,7},{6,4},{7,5},{8,72},{9,73},... | collective-permute-start | bytes 1572872 | tf_op jit(solution)/shard_map/ppermute | solution.py:250
  12.4 11.5 %collective-permute-start.2 = (f32[256,512]{1,0:T(8,128)S(1)}, f32[256,512]{1,0:T(8,128)S(1)}, u32[]{:S(2)}, u32[]{:S(2)}) collective-permute-start(f32[256,512]{1,0:T(8,128)S(1)} %shard_map.68), channel_id=1, source_target_pairs={{0,96},{1,97},{2,98},{3,99},{4,7},{5,6},{6,5},{7,4},{8,104},{9,105... | collective-permute-start | bytes 1572872 | tf_op jit(solution)/shard_map/ppermute | solution.py:250
  14.5 10.5 %collective-permute-start.3 = (f32[256,512]{1,0:T(8,128)S(1)}, f32[256,512]{1,0:T(8,128)S(1)}, u32[]{:S(2)}, u32[]{:S(2)}) collective-permute-start(f32[256,512]{1,0:T(8,128)S(1)} %shard_map.70), channel_id=1, source_target_pairs={{0,32},{1,33},{2,34},{3,35},{4,5},{5,4},{6,7},{7,6},{8,40},{9,41},... | collective-permute-start | bytes 1572872 | tf_op jit(solution)/shard_map/ppermute | solution.py:252
  17.2 25.1 %copy-start = (bf16[512,1024]{1,0:T(8,128)(2,1)S(1)}, bf16[512,1024]{1,0:T(8,128)(2,1)}, u32[]{:S(2)}) copy-start(bf16[512,1024]{1,0:T(8,128)(2,1)} %constant.14.clone.t_low) | copy-start | bytes 3145732
  17.2 25.0 %copy-start.1 = (bf16[512,1024]{1,0:T(8,128)(2,1)S(1)}, bf16[512,1024]{1,0:T(8,128)(2,1)}, u32[]{:S(2)}) copy-start(bf16[512,1024]{1,0:T(8,128)(2,1)} %constant.13.clone.t_high) | copy-start | bytes 3145732
  25.1 8.4 %collective-permute-start.4 = (f32[64,512]{1,0:T(8,128)S(1)}, f32[64,512]{1,0:T(8,128)S(1)}, u32[]{:S(2)}, u32[]{:S(2)}) collective-permute-start(f32[64,512]{1,0:T(8,128)S(1)} %get-tuple-element.32), channel_id=1, source_target_pairs={{0,27},{1,26},{2,25},{3,24},{4,68},{5,69},{6,70},{7,71},{8,19},{9,... | collective-permute-start | bytes 393224 | tf_op jit(solution)/shard_map/ppermute | solution.py:254
  30.4 6.2 %collective-permute-start.5 = (f32[64,512]{1,0:T(8,128)S(1)}, f32[64,512]{1,0:T(8,128)S(1)}, u32[]{:S(2)}, u32[]{:S(2)}) collective-permute-start(f32[64,512]{1,0:T(8,128)S(1)} %get-tuple-element.33), channel_id=1, source_target_pairs={{0,24},{1,25},{2,26},{3,27},{4,100},{5,101},{6,102},{7,103},{8,16}... | collective-permute-start | bytes 393224 | tf_op jit(solution)/shard_map/ppermute | solution.py:254
  30.6 6.2 %collective-permute-start.6 = (f32[64,512]{1,0:T(8,128)S(1)}, f32[64,512]{1,0:T(8,128)S(1)}, u32[]{:S(2)}, u32[]{:S(2)}) collective-permute-start(f32[64,512]{1,0:T(8,128)S(1)} %get-tuple-element.34), channel_id=1, source_target_pairs={{0,3},{1,2},{2,1},{3,0},{4,36},{5,37},{6,38},{7,39},{8,11},{9,10},... | collective-permute-start | bytes 393224 | tf_op jit(solution)/shard_map/ppermute | solution.py:254
  36.8 4.9 %collective-permute-start.7 = (f32[16,512]{1,0:T(8,128)S(1)}, f32[16,512]{1,0:T(8,128)S(1)}, u32[]{:S(2)}, u32[]{:S(2)}) collective-permute-start(f32[16,512]{1,0:T(8,128)S(1)} %get-tuple-element.36), channel_id=1, source_target_pairs={{0,9},{1,8},{2,11},{3,10},{4,20},{5,21},{6,22},{7,23},{8,1},{9,0},... | collective-permute-start | bytes 98312 | tf_op jit(solution)/shard_map/ppermute | solution.py:256
  36.9 4.8 %collective-permute-start.8 = (f32[16,512]{1,0:T(8,128)S(1)}, f32[16,512]{1,0:T(8,128)S(1)}, u32[]{:S(2)}, u32[]{:S(2)}) collective-permute-start(f32[16,512]{1,0:T(8,128)S(1)} %get-tuple-element.37), channel_id=1, source_target_pairs={{0,8},{1,9},{2,10},{3,11},{4,28},{5,29},{6,30},{7,31},{8,0},{9,1},... | collective-permute-start | bytes 98312 | tf_op jit(solution)/shard_map/ppermute | solution.py:256
  38.4 3.9 %collective-permute-start.9 = (f32[16,512]{1,0:T(8,128)S(1)}, f32[16,512]{1,0:T(8,128)S(1)}, u32[]{:S(2)}, u32[]{:S(2)}) collective-permute-start(f32[16,512]{1,0:T(8,128)S(1)} %get-tuple-element.38), channel_id=1, source_target_pairs={{0,1},{1,0},{2,3},{3,2},{4,12},{5,13},{6,14},{7,15},{8,9},{9,8},{1... | collective-permute-start | bytes 98312 | tf_op jit(solution)/shard_map/ppermute | solution.py:256

commit v4 on v3

--- a/solution.py
+++ b/solution.py
@@ -77,7 +77,7 @@
     c, s = ct.reshape(tiles, 8, 128), st.reshape(tiles, 8, 128)
     for at in range(0, wc.shape[1], 128):
         a, b = wc[:, at : at + 128][:, None, :], ws[:, at : at + 128][:, None, :]
-        both = jnp.concatenate([a * c - b * s, -(a * s + b * c)], axis=1)
+        both = jnp.concatenate([a * c + b * s, a * s - b * c], axis=1)
         high[:, at : at + 128], low[:, at : at + 128] = halves(both.reshape(tiles * 16, 128))
 
 
@@ -87,7 +87,7 @@
 
 def own_kernel(
     where, frames_in, masks_in, aperture_in, phases_in, part, wc, ws, ct, st, ct2, st2, f_high, f_low,
-    frames, masks, aperture, phases, a_high, a_low, sems,
+    frames, masks, aperture, phases, sems, *matrices,
 ):
     pieces = [pl.ds(at * 128, 128) for at in range(8)]
     pairs = [(masks_in, masks), (aperture_in, aperture), (phases_in, phases)]
@@ -134,14 +134,20 @@
         c2, s2 = turn(iota((8, 128), 0) * row & 1023)
         c1, s1 = c1[:, None, :], s1[:, None, :]
         c_out[...] = (c1 * c2[None] - s1 * s2[None]).reshape(512, 128)
-        s_out[...] = (s1 * c2[None] + c1 * s2[None]).reshape(512, 128)
+        s_out[...] = -(s1 * c2[None] + c1 * s2[None]).reshape(512, 128)
     for piece, copy in zip(pieces, copies[3:]):
         copy.wait()
         f_high[piece, :], f_low[piece, :] = halves(frames[piece, :])
+
+    def fill(step):
+        tiles, rows = slice(step * 16, step * 16 + 16), slice(step * 128, step * 128 + 128)
+        fill_matrix(wc[tiles, :], ws[tiles, :], ct[rows, :], st[rows, :], *matrices[2 * step - 2 : 2 * step])
+
+    fill(1)
     for step in (1, 2, 3):
-        tiles, rows = slice(step * 16, step * 16 + 16), slice(step * 128, step * 128 + 128)
-        high, low = a_high.at[step - 1], a_low.at[step - 1]
-        fill_matrix(wc[tiles, :], ws[tiles, :], ct[rows, :], st[rows, :], high, low)
+        if step < 3:
+            fill(step + 1)
+        high, low = matrices[2 * step - 2 : 2 * step]
         part[step * 256 : step * 256 + 256, :] = product(high, low, f_high, f_low)
 
 
@@ -226,8 +232,8 @@
             pltpu.VMEM((1, 128), jnp.int32),
             pltpu.VMEM((1, 256), jnp.float32),
         ]
-        + [pltpu.VMEM((3, 256, 1024), jnp.bfloat16)] * 2
-        + [pltpu.SemaphoreType.DMA((11,))],
+        + [pltpu.SemaphoreType.DMA((11,))]
+        + [pltpu.VMEM((256, 1024), jnp.bfloat16)] * 6,
         cost_estimate=pl.CostEstimate(flops=6 * 768 * 1024 * 512, bytes_accessed=5 << 20, transcendentals=0),
         compiler_params=pltpu.CompilerParams(vmem_limit_bytes=24 << 20),
     )(where, *[pltpu.with_memory_space_constraint(u, pltpu.HBM) for u in (frames.reshape(1024, col_len), intersection_masks, aperture[None, :], phases[None, :])])

time: 43.9 us -> 43.8 us (level)
  no operation moved by 1% of the time
where the time goes in v4:
time: 43.8 us; the launch traced here: 43.3 us
  waiting for transfers between devices  15.3 us (35%)
  starting transfers between devices  14.8 us (34%)
  Pallas kernels  13 us (30%)
    ppermute x2, waiting for transfers between devices, body(): got = lax.ppermute(send[step], AXES, partners(0, step - 1))  6.73 us
    ppermute x3, starting transfers between devices, body(): lax.ppermute(send[step], AXES, partners(1, step - 1))  5.99 us
    pallas_call x1, Pallas kernels, body(): pl.pallas_call(own_kernel, out_shape=[f32(1024, col_len)] + [f32(64, 1024...  5.77 us
    ppermute x3, waiting for transfers between devices, body(): lax.ppermute(send[step], AXES, partners(1, step - 1))  5.7 us
    ppermute x2, starting transfers between devices, body(): got = lax.ppermute(send[step], AXES, partners(0, step - 1))  4.83 us
    pallas_call x3, Pallas kernels, body(): call(functools.partial(later_kernel, step), block, scratch, inputs=6, **c...  3.68 us
    ppermute x3, starting transfers between devices, body(): lax.ppermute(send[step], AXES, partners(2, step - 1))  3.56 us
    pallas_call x1, Pallas kernels, body(): call(near_kernel, block, scratch, inputs=9, **cost)  2.3 us
  transfers between devices with their start and end apart: 10, of which 8 were waited for; matrix products, arithmetic and copies ran while one was open for 0% of the time, Pallas kernels for 25%

profile of v4, /device:TPU:0, one launch (start us, length us, event | category | flops | bytes accessed | tf_op | source)
XLA Modules:
  0.0 43.3 jit_solution(17797806780946717942)
XLA Ops:
  0.0 0.0 collective-permute-start
  0.0 0.1 pad_add_fusion.where
  0.1 5.8 %shard_map.64 = (f32[1024,512]{1,0:T(8,128)S(1)}, f32[64,1024]{1,0:T(8,128)S(1)}, f32[64,1024]{1,0:T(8,128)S(1)}, f32[512,128]{1,0:T(8,128)S(1)}, f32[512,128]{1...) custom-call(s32[2]{0:T(128)S(1)} %pad_add_fusion.where, ...), custom_call_target="tpu_custom_call" | custom-call | flops 2415919104 | bytes 5242880 | tf_op jit(solution)/shard_map/pallas_call | solution.py:224
  5.9 0.0 collective-permute-done
  5.9 1.2 %shard_map.66 = f32[256,512]{1,0:T(8,128)S(1)} custom-call(f32[1024,512]{1,0:T(8,128)S(1)} %bitcast.6, f32[1024,512]{1,0:T(8,128)S(1)} %get-tuple-element.30.part, f32[64,1024]{1,0:T(8,128)S(1)} %get-tuple-element.24.wc, f32[64,1024]{1,0:T(8,128)S(1)} %get-tuple-element.25.ws, f32[512,128]{1,0:T(8,128)S(1)} %get-tuple-element.28.ct2.ct, ...), custom_call_target="tpu_custom_call" | custom-call | flops 1000 | bytes 1000 | tf_op jit(solution)/shard_map/pallas_call | solution.py:245
  7.1 4.0 %collective-permute-start.1 = (f32[256,512]{1,0:T(8,128)S(1)}, f32[256,512]{1,0:T(8,128)S(1)}, u32[]{:S(2)}, u32[]{:S(2)}) collective-permute-start(f32[256,512]{1,0:T(8,128)S(1)} %shard_map.66), channel_id=1, source_target_pairs={{0,64},{1,65},{2,66},{3,67},{4,6},{5,7},{6,4},{7,5},{8,72},{9,73},... | collective-permute-start | bytes 1572872 | tf_op jit(solution)/shard_map/ppermute | solution.py:256
  11.1 1.2 %shard_map.68 = f32[256,512]{1,0:T(8,128)S(1)} custom-call(f32[1024,512]{1,0:T(8,128)S(1)} %bitcast.7, f32[1024,512]{1,0:T(8,128)S(1)} %get-tuple-element.30.part, f32[64,1024]{1,0:T(8,128)S(1)} %get-tuple-element.24.wc, f32[64,1024]{1,0:T(8,128)S(1)} %get-tuple-element.25.ws, f32[512,128]{1,0:T(8,128)S(1)} %get-tuple-element.28.ct2.ct, ...), custom_call_target="tpu_custom_call" | custom-call | flops 1000 | bytes 1000 | tf_op jit(solution)/shard_map/pallas_call | solution.py:245
  12.4 0.8 %collective-permute-start.2 = (f32[256,512]{1,0:T(8,128)S(1)}, f32[256,512]{1,0:T(8,128)S(1)}, u32[]{:S(2)}, u32[]{:S(2)}) collective-permute-start(f32[256,512]{1,0:T(8,128)S(1)} %shard_map.68), channel_id=1, source_target_pairs={{0,96},{1,97},{2,98},{3,99},{4,7},{5,6},{6,5},{7,4},{8,104},{9,105... | collective-permute-start | bytes 1572872 | tf_op jit(solution)/shard_map/ppermute | solution.py:256
  13.2 1.2 %shard_map.70 = f32[256,512]{1,0:T(8,128)S(1)} custom-call(f32[1024,512]{1,0:T(8,128)S(1)} %bitcast.8, f32[1024,512]{1,0:T(8,128)S(1)} %get-tuple-element.30.part, f32[64,1024]{1,0:T(8,128)S(1)} %get-tuple-element.24.wc, f32[64,1024]{1,0:T(8,128)S(1)} %get-tuple-element.25.ws, f32[512,128]{1,0:T(8,128)S(1)} %get-tuple-element.28.ct2.ct, ...), custom_call_target="tpu_custom_call" | custom-call | flops 1000 | bytes 1000 | tf_op jit(solution)/shard_map/pallas_call | solution.py:245
  14.4 0.4 collective-permute-start.3
  14.8 2.3 %shard_map.65.a = f32[256,512]{1,0:T(8,128)S(1)} custom-call(bf16[1024,512]{1,0:T(8,128)(2,1)S(1)} %get-tuple-element.22.own_high, bf16[1024,512]{1,0:T(8,128)(2,1)S(1)} %get-tuple-element.23.own_low, f32[1024,512]{1,0:T(8,128)S(1)} %bitcast.9, f32[64,1024]{1,0:T(8,128)S(1)} %get-tuple-element.24.wc, f32[64,1024]{1,0:T(8,128)S(1)} %get-tuple-element.25.ws, ...), custom_call_target="tpu_custom_call" | custom-call | flops 1000 | bytes 1000 | tf_op jit(solution)/shard_map/pallas_call | solution.py:248
  17.1 0.0 copy-start
  17.1 0.0 copy-start.1
  17.1 1.3 %collective-permute-done.1.b = f32[256,512]{1,0:T(8,128)S(1)} collective-permute-done((f32[256,512]{1,0:T(8,128)S(1)}, f32[256,512]{1,0:T(8,128)S(1)}, u32[]{:S(2)}, u32[]{:S(2)}) %collective-permute-start.1) | collective-permute-done | bytes 524320 | tf_op jit(solution)/shard_map/ppermute | solution.py:256
  18.4 0.1 shard_map.67.a
  18.5 5.5 %collective-permute-done.2.b = f32[256,512]{1,0:T(8,128)S(1)} collective-permute-done((f32[256,512]{1,0:T(8,128)S(1)}, f32[256,512]{1,0:T(8,128)S(1)}, u32[]{:S(2)}, u32[]{:S(2)}) %collective-permute-start.2) | collective-permute-done | bytes 524320 | tf_op jit(solution)/shard_map/ppermute | solution.py:256
  23.9 0.1 shard_map.69.a
  24.0 1.0 %collective-permute-done.3.b = f32[256,512]{1,0:T(8,128)S(1)} collective-permute-done((f32[256,512]{1,0:T(8,128)S(1)}, f32[256,512]{1,0:T(8,128)S(1)}, u32[]{:S(2)}, u32[]{:S(2)}) %collective-permute-start.3) | collective-permute-done | bytes 524320 | tf_op jit(solution)/shard_map/ppermute | solution.py:258
  25.0 0.1 shard_map.71
  25.0 5.3 %collective-permute-start.4 = (f32[64,512]{1,0:T(8,128)S(1)}, f32[64,512]{1,0:T(8,128)S(1)}, u32[]{:S(2)}, u32[]{:S(2)}) collective-permute-start(f32[64,512]{1,0:T(8,128)S(1)} %get-tuple-element.32), channel_id=1, source_target_pairs={{0,27},{1,26},{2,25},{3,24},{4,68},{5,69},{6,70},{7,71},{8,19},{9,... | collective-permute-start | bytes 393224 | tf_op jit(solution)/shard_map/ppermute | solution.py:260
  30.3 0.2 collective-permute-start.5
  30.6 0.5 %collective-permute-start.6 = (f32[64,512]{1,0:T(8,128)S(1)}, f32[64,512]{1,0:T(8,128)S(1)}, u32[]{:S(2)}, u32[]{:S(2)}) collective-permute-start(f32[64,512]{1,0:T(8,128)S(1)} %get-tuple-element.34), channel_id=1, source_target_pairs={{0,3},{1,2},{2,1},{3,0},{4,36},{5,37},{6,38},{7,39},{8,11},{9,10},... | collective-permute-start | bytes 393224 | tf_op jit(solution)/shard_map/ppermute | solution.py:260
  31.0 2.4 %collective-permute-done.4.b = f32[64,512]{1,0:T(8,128)S(1)} collective-permute-done((f32[64,512]{1,0:T(8,128)S(1)}, f32[64,512]{1,0:T(8,128)S(1)}, u32[]{:S(2)}, u32[]{:S(2)}) %collective-permute-start.4) | collective-permute-done | bytes 131104 | tf_op jit(solution)/shard_map/ppermute | solution.py:260
  33.4 3.1 %collective-permute-done.5.c = f32[64,512]{1,0:T(8,128)S(1)} collective-permute-done((f32[64,512]{1,0:T(8,128)S(1)}, f32[64,512]{1,0:T(8,128)S(1)}, u32[]{:S(2)}, u32[]{:S(2)}) %collective-permute-start.5) | collective-permute-done | bytes 131104 | tf_op jit(solution)/shard_map/ppermute | solution.py:260
  36.5 0.2 collective-permute-done.6.d
  36.8 0.1 collective-permute-start.7
  36.9 1.5 %collective-permute-start.8 = (f32[16,512]{1,0:T(8,128)S(1)}, f32[16,512]{1,0:T(8,128)S(1)}, u32[]{:S(2)}, u32[]{:S(2)}) collective-permute-start(f32[16,512]{1,0:T(8,128)S(1)} %get-tuple-element.37), channel_id=1, source_target_pairs={{0,8},{1,9},{2,10},{3,11},{4,28},{5,29},{6,30},{7,31},{8,0},{9,1},... | collective-permute-start | bytes 98312 | tf_op jit(solution)/shard_map/ppermute | solution.py:262
  38.3 2.0 %collective-permute-start.9 = (f32[16,512]{1,0:T(8,128)S(1)}, f32[16,512]{1,0:T(8,128)S(1)}, u32[]{:S(2)}, u32[]{:S(2)}) collective-permute-start(f32[16,512]{1,0:T(8,128)S(1)} %get-tuple-element.38), channel_id=1, source_target_pairs={{0,1},{1,0},{2,3},{3,2},{4,12},{5,13},{6,14},{7,15},{8,9},{9,8},{1... | collective-permute-start | bytes 98312 | tf_op jit(solution)/shard_map/ppermute | solution.py:262
  40.3 1.3 %collective-permute-done.7.b = f32[16,512]{1,0:T(8,128)S(1)} collective-permute-done((f32[16,512]{1,0:T(8,128)S(1)}, f32[16,512]{1,0:T(8,128)S(1)}, u32[]{:S(2)}, u32[]{:S(2)}) %collective-permute-start.7) | collective-permute-done | bytes 32800 | tf_op jit(solution)/shard_map/ppermute | solution.py:262
  41.7 0.0 collective-permute-done.8.c
  41.7 0.6 %collective-permute-done.9.d = f32[16,512]{1,0:T(8,128)S(1)} collective-permute-done((f32[16,512]{1,0:T(8,128)S(1)}, f32[16,512]{1,0:T(8,128)S(1)}, u32[]{:S(2)}, u32[]{:S(2)}) %collective-permute-start.9) | collective-permute-done | bytes 32800 | tf_op jit(solution)/shard_map/ppermute | solution.py:262
  42.2 0.0 copy-done
  42.2 0.0 copy-done.1
  42.2 1.0 %shard_map.73 = f32[8,2,512]{2,1,0:T(2,128)} custom-call(f32[16,512]{1,0:T(8,128)S(1)} %get-tuple-element.35.a, f32[16,512]{1,0:T(8,128)S(1)} %collective-permute-done.7.b, f32[16,512]{1,0:T(8,128)S(1)} %collective-permute-done.8.c, f32[16,512]{1,0:T(8,128)S(1)} %collective-permute-done.9.d, bf16[512,1024]{1,0:T(8,128)(2,1)S(1)} %copy-done.1, ...), custom_call_target="tpu_custom_call" | custom-call | flops 67108864 | bytes 2097152 | tf_op jit(solution)/shard_map/pallas_call | solution.py:263
  (1 shorter events, 0.0 us)
Async XLA Ops:
  0.0 5.9 %collective-permute-start = (f32[32,32,512]{2,1,0:T(8,128)}, f32[32,32,512]{2,1,0:T(8,128)S(1)}, u32[]{:S(2)}, u32[]{:S(2)}) collective-permute-start(f32[32,32,512]{2,1,0:T(8,128)} %param.6), channel_id=1, source_target_pairs={{0,4},{1,5},{2,6},{3,7},{4,0},{5,1},{6,2},{7,3},{8,12},{9,13},{10,... | collective-permute-start | bytes 6291464 | tf_op jit(solution)/shard_map/ppermute | solution.py:222
  7.1 11.3 %collective-permute-start.1 = (f32[256,512]{1,0:T(8,128)S(1)}, f32[256,512]{1,0:T(8,128)S(1)}, u32[]{:S(2)}, u32[]{:S(2)}) collective-permute-start(f32[256,512]{1,0:T(8,128)S(1)} %shard_map.66), channel_id=1, source_target_pairs={{0,64},{1,65},{2,66},{3,67},{4,6},{5,7},{6,4},{7,5},{8,72},{9,73},... | collective-permute-start | bytes 1572872 | tf_op jit(solution)/shard_map/ppermute | solution.py:256
  12.4 11.5 %collective-permute-start.2 = (f32[256,512]{1,0:T(8,128)S(1)}, f32[256,512]{1,0:T(8,128)S(1)}, u32[]{:S(2)}, u32[]{:S(2)}) collective-permute-start(f32[256,512]{1,0:T(8,128)S(1)} %shard_map.68), channel_id=1, source_target_pairs={{0,96},{1,97},{2,98},{3,99},{4,7},{5,6},{6,5},{7,4},{8,104},{9,105... | collective-permute-start | bytes 1572872 | tf_op jit(solution)/shard_map/ppermute | solution.py:256
  14.4 10.6 %collective-permute-start.3 = (f32[256,512]{1,0:T(8,128)S(1)}, f32[256,512]{1,0:T(8,128)S(1)}, u32[]{:S(2)}, u32[]{:S(2)}) collective-permute-start(f32[256,512]{1,0:T(8,128)S(1)} %shard_map.70), channel_id=1, source_target_pairs={{0,32},{1,33},{2,34},{3,35},{4,5},{5,4},{6,7},{7,6},{8,40},{9,41},... | collective-permute-start | bytes 1572872 | tf_op jit(solution)/shard_map/ppermute | solution.py:258
  17.1 25.1 %copy-start = (bf16[512,1024]{1,0:T(8,128)(2,1)S(1)}, bf16[512,1024]{1,0:T(8,128)(2,1)}, u32[]{:S(2)}) copy-start(bf16[512,1024]{1,0:T(8,128)(2,1)} %constant.14.clone.t_low) | copy-start | bytes 3145732
  17.1 25.1 %copy-start.1 = (bf16[512,1024]{1,0:T(8,128)(2,1)S(1)}, bf16[512,1024]{1,0:T(8,128)(2,1)}, u32[]{:S(2)}) copy-start(bf16[512,1024]{1,0:T(8,128)(2,1)} %constant.13.clone.t_high) | copy-start | bytes 3145732
  25.0 8.4 %collective-permute-start.4 = (f32[64,512]{1,0:T(8,128)S(1)}, f32[64,512]{1,0:T(8,128)S(1)}, u32[]{:S(2)}, u32[]{:S(2)}) collective-permute-start(f32[64,512]{1,0:T(8,128)S(1)} %get-tuple-element.32), channel_id=1, source_target_pairs={{0,27},{1,26},{2,25},{3,24},{4,68},{5,69},{6,70},{7,71},{8,19},{9,... | collective-permute-start | bytes 393224 | tf_op jit(solution)/shard_map/ppermute | solution.py:260
  30.3 6.2 %collective-permute-start.5 = (f32[64,512]{1,0:T(8,128)S(1)}, f32[64,512]{1,0:T(8,128)S(1)}, u32[]{:S(2)}, u32[]{:S(2)}) collective-permute-start(f32[64,512]{1,0:T(8,128)S(1)} %get-tuple-element.33), channel_id=1, source_target_pairs={{0,24},{1,25},{2,26},{3,27},{4,100},{5,101},{6,102},{7,103},{8,16}... | collective-permute-start | bytes 393224 | tf_op jit(solution)/shard_map/ppermute | solution.py:260
  30.6 6.2 %collective-permute-start.6 = (f32[64,512]{1,0:T(8,128)S(1)}, f32[64,512]{1,0:T(8,128)S(1)}, u32[]{:S(2)}, u32[]{:S(2)}) collective-permute-start(f32[64,512]{1,0:T(8,128)S(1)} %get-tuple-element.34), channel_id=1, source_target_pairs={{0,3},{1,2},{2,1},{3,0},{4,36},{5,37},{6,38},{7,39},{8,11},{9,10},... | collective-permute-start | bytes 393224 | tf_op jit(solution)/shard_map/ppermute | solution.py:260
  36.8 4.9 %collective-permute-start.7 = (f32[16,512]{1,0:T(8,128)S(1)}, f32[16,512]{1,0:T(8,128)S(1)}, u32[]{:S(2)}, u32[]{:S(2)}) collective-permute-start(f32[16,512]{1,0:T(8,128)S(1)} %get-tuple-element.36), channel_id=1, source_target_pairs={{0,9},{1,8},{2,11},{3,10},{4,20},{5,21},{6,22},{7,23},{8,1},{9,0},... | collective-permute-start | bytes 98312 | tf_op jit(solution)/shard_map/ppermute | solution.py:262
  36.9 4.8 %collective-permute-start.8 = (f32[16,512]{1,0:T(8,128)S(1)}, f32[16,512]{1,0:T(8,128)S(1)}, u32[]{:S(2)}, u32[]{:S(2)}) collective-permute-start(f32[16,512]{1,0:T(8,128)S(1)} %get-tuple-element.37), channel_id=1, source_target_pairs={{0,8},{1,9},{2,10},{3,11},{4,28},{5,29},{6,30},{7,31},{8,0},{9,1},... | collective-permute-start | bytes 98312 | tf_op jit(solution)/shard_map/ppermute | solution.py:262
  38.3 3.9 %collective-permute-start.9 = (f32[16,512]{1,0:T(8,128)S(1)}, f32[16,512]{1,0:T(8,128)S(1)}, u32[]{:S(2)}, u32[]{:S(2)}) collective-permute-start(f32[16,512]{1,0:T(8,128)S(1)} %get-tuple-element.38), channel_id=1, source_target_pairs={{0,1},{1,0},{2,3},{3,2},{4,12},{5,13},{6,14},{7,15},{8,9},{9,8},{1... | collective-permute-start | bytes 98312 | tf_op jit(solution)/shard_map/ppermute | solution.py:262
